TPU v7x, 1024 devices: a whole 4x8x16 slice. The times are simulated.
1024 devices in a mesh: vel: 16 (over x_hi, y), space: 64 (over z, x_lo, core).
Axes of the slice: x: 4 (x_hi: 2, x_lo: 2; x = x_hi * 2 + x_lo), y: 8, z: 16, core: 2. Of those that a mesh axis runs over, the one named last changes fastest.
Arguments:
- distribution: float32 [4096, 32768], P('vel', 'space'), may hold values from -6 to 6
- cell_kind: int32 [32768], P('space'), may hold values from 0 to 3
- type_rates: float32 [4], replicated, may hold values from 0.2 to 1
- mode_weights: float32 [512], replicated, may hold values from 0.05 to 1
Outputs:
- result: float32 [4096, 32768], P('vel', 'space')
Inputs may be any that keep to these rules, and one draw needn't show every extreme that they name: `cell_kind`: each cell's class.
All inputs are finite; a program needn't handle non-finite values.
Results may differ from a plain program's by a relative error of at most 0.0003.
Values sent between devices are 32-bit elements; how exact they have to be, the bound alone decides.
No kernel may reach another device: no remote copies, remote signals or barrier semaphores. Data moves between devices by JAX's collectives and lax.ppermute only.
A program may use at most 32 MiB of HBM per device.

v0:
```python
import math

import jax
import jax.numpy as jnp
from jax import lax
from jax.sharding import PartitionSpec as P

V = 4096
K = 512
STEPS = 2


courant_limit = 0.9


def extended(block, sides, width):
    for axis, dim in sides:
        count = lax.axis_size(axis)
        forward = [(i, i + 1) for i in range(count - 1)]
        forward.append((count - 1, 0))
        backward = [(target, source) for source, target in forward]
        low = lax.ppermute(
            lax.slice_in_dim(block, block.shape[dim] - width, None, axis=dim), axis, forward
        )
        high = lax.ppermute(lax.slice_in_dim(block, 0, width, axis=dim), axis, backward)
        block = jnp.concatenate([low, block, high], axis=dim)
    return block


def minmod(first_term, second_term):
    lower = jnp.where(
        first_term > 0.0, jnp.minimum(first_term, second_term), jnp.maximum(first_term, second_term)
    )
    return jnp.where(first_term * second_term > 0.0, lower, jnp.zeros_like(first_term))


def advect(padded, courant):
    width = padded.shape[1] - 4
    differences = padded[:, 1:] - padded[:, :-1]
    slopes = minmod(differences[:, :-1], differences[:, 1:])
    left_face = padded[:, 1 : width + 2] + 0.5 * (1.0 - courant) * slopes[:, 0 : width + 1]
    right_face = padded[:, 2 : width + 3] - 0.5 * (1.0 + courant) * slopes[:, 1 : width + 2]
    face_values = jnp.where(courant > 0.0, left_face, right_face)
    return padded[:, 2 : width + 2] - courant * (face_values[:, 1:] - face_values[:, :-1])


def courant_numbers(first_velocity, velocity_count):
    velocity_index = first_velocity + jnp.arange(velocity_count, dtype=jnp.int32)
    return ((2 * velocity_index + 1 - V).astype(jnp.float32) * (courant_limit / V))[:, None]


def cosine_factors(first_velocity, velocity_count):
    velocity_index = first_velocity + jnp.arange(velocity_count, dtype=jnp.int32)
    modes = jnp.arange(K, dtype=jnp.int32)
    phase_index = (2 * velocity_index + 1)[:, None] * modes[None, :] % (4 * V)
    phase_angle = phase_index.astype(jnp.float32) * (math.pi / (2 * V))
    column_scale = jnp.where(modes == 0, math.sqrt(1.0 / V), math.sqrt(2.0 / V))
    return jnp.cos(phase_angle) * column_scale[None, :]


def rates_of_cells(cell_kind, type_rates):
    kinds = jnp.arange(type_rates.shape[0], dtype=jnp.int32)
    match = (cell_kind[None, :] == kinds[:, None]).astype(jnp.float32)
    return jnp.sum(match * type_rates[:, None], axis=0)


def contract_first(left_matrix, right_matrix):
    return lax.dot_general(
        left_matrix,
        right_matrix,
        (((0,), (0,)), ((), ())),
        precision=lax.Precision.HIGHEST,
        preferred_element_type=jnp.float32,
    )


def contract_last(left_matrix, right_matrix):
    return lax.dot_general(
        left_matrix,
        right_matrix,
        (((1,), (1,)), ((), ())),
        precision=lax.Precision.HIGHEST,
        preferred_element_type=jnp.float32,
    )


def shards(distribution, cell_kind, type_rates, mode_weights):
    local_velocities = distribution.shape[0]
    first_velocity = lax.axis_index("vel") * local_velocities
    courant = courant_numbers(first_velocity, local_velocities)
    cell_rates = rates_of_cells(cell_kind, type_rates)
    factors = cosine_factors(first_velocity, local_velocities)
    for time_step in range(STEPS):
        padded = extended(distribution, (("space", 1),), 2)
        advected = advect(padded, courant)
        mode_shares = lax.psum_scatter(
            contract_first(advected, factors), "vel", scatter_dimension=0, tiled=True
        )
        scaled = mode_shares * mode_weights[None, :]
        change = contract_last(factors, lax.all_gather(scaled, "vel", axis=0, tiled=True))
        distribution = advected - cell_rates[None, :] * change
    return distribution


def solution(mesh):
    return jax.shard_map(
        shards,
        mesh=mesh,
        in_specs=(P("vel", "space"), P("space"), P(), P()),
        out_specs=P("vel", "space"),
        check_vma=False,
    )
```

profile of v0, /device:TPU:16, one launch (start us, length us, event | category | flops | bytes accessed | tf_op | source)
XLA Modules:
  0.0 690.6 jit_solution(352283857990481491)
XLA Ops:
  6.5 1.1 fusion.45
  7.7 1.9 collective-permute-start
  9.6 18.6 %collective-permute-start.1 = (f32[256,2]{1,0:T(8,128)S(1)}, f32[256,2]{1,0:T(8,128)S(1)}, u32[]{:S(2)}, u32[]{:S(2)}) collective-permute-start(f32[256,2]{1,0:T(8,128)S(1)} %get-tuple-element.8), channel_id=1, source_target_pairs={{1,0},{2,1},{3,2},{4,3},{5,4},{6,5},{7,6},{8,7},{9,8},{10,9},{11,1... | collective-permute-start | bytes 6152 | tf_op jit(solution)/shard_map/ppermute | solution.py:25
  28.3 0.6 collective-permute-done
  28.9 1.8 collective-permute-done.1
  30.7 0.3 pad_maximum_fusion.4
  31.5 0.6 fusion.6
  32.3 4.0 fusion.24
  36.5 212.7 %reduce-scatter.3.cloned.1.call-done = f32[32,512]{1,0:T(8,128)} async-done(((f32[512,512]{1,0:T(8,128)}), f32[32,512]{1,0:T(8,128)}) %reduce-scatter.3.cloned.1.call-update) | async-done | bytes 65552 | tf_op jit(solution)/shard_map/reduce_scatter | solution.py:96
  249.2 1.5 broadcast_multiply_fusion.1
  250.8 0.6 copy-done.2
  251.4 94.8 %all-gather.3.cloned.1.call-done = f32[512,512]{1,0:T(8,128)} async-done(((f32[32,512]{1,0:T(8,128)}), f32[512,512]{1,0:T(8,128)}) %all-gather.3.cloned.1.call-update) | async-done | bytes 1048592 | tf_op jit(solution)/shard_map/all_gather | solution.py:100
  346.2 4.3 fusion
  350.6 1.9 collective-permute-start.2
  352.6 5.9 collective-permute-start.3
  358.5 0.6 collective-permute-done.2
  359.1 1.7 collective-permute-done.3
  360.8 0.3 pad_maximum_fusion.5
  361.6 0.6 fusion.3
  362.4 4.0 fusion.21
  366.5 215.6 %reduce-scatter.5.cloned.1.call-done = f32[32,512]{1,0:T(8,128)} async-done(((f32[512,512]{1,0:T(8,128)}), f32[32,512]{1,0:T(8,128)}) %reduce-scatter.5.cloned.1.call-update) | async-done | bytes 65552 | tf_op jit(solution)/shard_map/reduce_scatter | solution.py:96
  582.1 1.5 broadcast_multiply_fusion
  583.6 95.3 %all-gather.5.cloned.1.call-done = f32[512,512]{1,0:T(8,128)} async-done(((f32[32,512]{1,0:T(8,128)}), f32[512,512]{1,0:T(8,128)}) %all-gather.5.cloned.1.call-update) | async-done | bytes 1048592 | tf_op jit(solution)/shard_map/all_gather | solution.py:100
  678.9 5.1 fusion.1
  (28 shorter events, 1.9 us)
Async XLA Ops:
  6.5 24.2 %copy-start = (f32[256,512]{1,0:T(8,128)S(1)}, f32[256,512]{1,0:T(8,128)}, u32[]{:S(2)}) copy-start(f32[256,512]{1,0:T(8,128)} %param.4) | copy-start | bytes 1572868
  6.5 242.7 %reduce-scatter.3.cloned.1.call-start = ((), (), s32[]{:S(2)}) async-start(), calls=%async_computation.2 | async-start | bytes 1114112 | tf_op jit(solution)/shard_map/reduce_scatter | solution.py:96
  7.7 21.2 %collective-permute-start = (f32[256,2]{1,0:T(8,128)S(1)}, f32[256,2]{1,0:T(8,128)S(1)}, u32[]{:S(2)}, u32[]{:S(2)}) collective-permute-start(f32[256,2]{1,0:T(8,128)S(1)} %get-tuple-element.7), channel_id=1, source_target_pairs={{0,1},{1,2},{2,3},{3,4},{4,5},{5,6},{6,7},{7,8},{8,9},{9,10},{10,1... | collective-permute-start | bytes 6152 | tf_op jit(solution)/shard_map/ppermute | solution.py:22
  9.6 21.1 %collective-permute-start.1 = (f32[256,2]{1,0:T(8,128)S(1)}, f32[256,2]{1,0:T(8,128)S(1)}, u32[]{:S(2)}, u32[]{:S(2)}) collective-permute-start(f32[256,2]{1,0:T(8,128)S(1)} %get-tuple-element.8), channel_id=1, source_target_pairs={{1,0},{2,1},{3,2},{4,3},{5,4},{6,5},{7,6},{8,7},{9,8},{10,9},{11,1... | collective-permute-start | bytes 6152 | tf_op jit(solution)/shard_map/ppermute | solution.py:25
  36.4 212.8 %copy-start.1 = (f32[512]{0:T(512)S(1)}, f32[512]{0:T(512)}, u32[]{:S(2)}) copy-start(f32[512]{0:T(512)} %param.7) | copy-start | bytes 6148
  36.4 309.8 %all-gather.3.cloned.1.call-start = ((), (), s32[]{:S(2)}) async-start(), calls=%async_computation.3 | async-start | bytes 1114112 | tf_op jit(solution)/shard_map/all_gather | solution.py:100
  250.7 0.7 copy-start.2
  250.7 0.7 copy-start.3
  250.7 331.4 %reduce-scatter.5.cloned.1.call-start = ((), (), s32[]{:S(2)}) async-start(), calls=%async_computation.4 | async-start | bytes 1114112 | tf_op jit(solution)/shard_map/reduce_scatter | solution.py:96
  350.6 8.5 %collective-permute-start.2 = (f32[256,2]{1,0:T(8,128)S(1)}, f32[256,2]{1,0:T(8,128)S(1)}, u32[]{:S(2)}, u32[]{:S(2)}) collective-permute-start(f32[256,2]{1,0:T(8,128)S(1)} %get-tuple-element.5), channel_id=1, source_target_pairs={{0,1},{1,2},{2,3},{3,4},{4,5},{5,6},{6,7},{7,8},{8,9},{9,10},{10,1... | collective-permute-start | bytes 6152 | tf_op jit(solution)/shard_map/ppermute | solution.py:22
  352.6 8.3 %collective-permute-start.3 = (f32[256,2]{1,0:T(8,128)S(1)}, f32[256,2]{1,0:T(8,128)S(1)}, u32[]{:S(2)}, u32[]{:S(2)}) collective-permute-start(f32[256,2]{1,0:T(8,128)S(1)} %get-tuple-element.6), channel_id=1, source_target_pairs={{1,0},{2,1},{3,2},{4,3},{5,4},{6,5},{7,6},{8,7},{9,8},{10,9},{11,1... | collective-permute-start | bytes 6152 | tf_op jit(solution)/shard_map/ppermute | solution.py:25
  366.5 312.4 %all-gather.5.cloned.1.call-start = ((), (), s32[]{:S(2)}) async-start(), calls=%async_computation.5 | async-start | bytes 1114112 | tf_op jit(solution)/shard_map/all_gather | solution.py:100
Sparse Core Ops, SparseCore 0:
  36.5 212.6 reduce-scatter.2
  253.5 92.6 all-gather.2
  366.6 215.4 reduce-scatter.4
  586.3 92.5 all-gather.4
where the time goes:
time: 691 us
  waiting for transfers between devices  623 us (90%)
  starting transfers between devices  28.5 us (4%)
  matrix products  17.5 us (3%)
  between operations  13.3 us (2%)
    reduce_scatter x2, waiting for transfers between devices, shards(): lax.psum_scatter(contract_first(advected, factors), 'vel', scatter_dimens...  428 us
    all_gather x2, waiting for transfers between devices, shards(): lax.all_gather(scaled, 'vel', axis=0, tiled=True)  190 us
    ppermute x2, starting transfers between devices, extended(): lax.ppermute(lax.slice_in_dim(block, 0, width, axis=dim), axis, backward)  24.5 us
  transfers between devices with their start and end apart: 8, of which 8 were waited for; matrix products, arithmetic and copies ran while one was open for 0% of the time, Pallas kernels for 0%

commit v1 on v0

v1 whole, which is shorter than its diff:
```python
import functools
import math

import jax
import jax.numpy as jnp
import numpy as np
from jax import lax
from jax.experimental import pallas as pl
from jax.experimental.pallas import tpu as pltpu
from jax.sharding import PartitionSpec as P

V = 4096
K = 512
B = 64
courant_limit = 0.9
F32 = jnp.float32
BF16 = jnp.bfloat16


def tables():
    k = np.arange(K)
    scale = np.where(k == 0, math.sqrt(1.0 / V), math.sqrt(2.0 / V))
    fine = (2 * np.arange(B) + 1)[:, None] * k[None, :] % (4 * V) * (math.pi / (2 * V))
    coarse = (2 * B * np.arange(V // B))[:, None] * k[None, :] % (4 * V) * (math.pi / (2 * V))
    parts = (np.cos(fine) * scale, np.sin(fine) * scale, np.cos(coarse), np.sin(coarse))
    return [part.astype(np.float32) for part in parts]


def split(x):
    hi = x.astype(BF16)
    return hi, (x - hi.astype(F32)).astype(BF16)


def dot(a, b):
    return lax.dot_general(a, b, (((1,), (0,)), ((), ())), preferred_element_type=F32)


def dot_t(a, b):
    return lax.dot_general(a, b, (((1,), (1,)), ((), ())), preferred_element_type=F32)


def minmod(a, b):
    zero = jnp.zeros_like(a)
    return jnp.minimum(jnp.maximum(a, zero), jnp.maximum(b, zero)) + jnp.maximum(
        jnp.minimum(a, zero), jnp.minimum(b, zero)
    )


def advect(padded, courant):
    width = padded.shape[0] - 4
    differences = padded[1:] - padded[:-1]
    slopes = minmod(differences[:-1], differences[1:])
    left_face = padded[1 : width + 2] + 0.5 * (1.0 - courant) * slopes[0 : width + 1]
    right_face = padded[2 : width + 3] - 0.5 * (1.0 + courant) * slopes[1 : width + 2]
    face = jnp.where(courant > 0.0, left_face, right_face)
    return padded[2 : width + 2] - courant * (face[1:] - face[:-1])


def courant_row(first, count):
    v = first + lax.broadcasted_iota(jnp.int32, (1, count), 1)
    return (2 * v + 1 - V).astype(F32) * (courant_limit / V)


def flip_kernel(rates_ref, f_ref, kind_ref, t_ref, first_ref, last_ref):
    kinds = kind_ref[...]
    rate = jnp.zeros(kinds.shape, F32)
    for j in range(rates_ref.shape[1]):
        rate = jnp.where(kinds == j, rates_ref[0, j], rate)
    nv, nx = f_ref.shape
    t_ref[:, :nv] = f_ref[...].T
    t_ref[:, nv:] = jnp.broadcast_to(rate, (128, nx)).T
    first_ref[...] = t_ref[:4, :]
    last_ref[...] = t_ref[nx - 4 :, :]


def factor_kernel(fc_ref, fs_ref, cc_ref, cs_ref, hi_ref, lo_ref):
    def body(a, carry):
        f = fc_ref[...] * cc_ref[pl.ds(a, 1), :] - fs_ref[...] * cs_ref[pl.ds(a, 1), :]
        hi, lo = split(f)
        rows = pl.ds(pl.multiple_of(a * B, B), B)
        hi_ref[rows, :] = hi
        lo_ref[rows, :] = lo
        return carry

    lax.fori_loop(0, V // B, body, 0)


def step_kernel(blocks, t_ref, low_ref, high_ref, out_ref, rate_ref, ext):
    me = lax.axis_index("vel")
    nx = t_ref.shape[0]
    nv = t_ref.shape[1] - 128
    own = nx // blocks
    wide = own + 4
    ext[:4, :] = low_ref[...]
    ext[4 : nx + 4, :] = t_ref[...]
    ext[nx + 4 :, :] = high_ref[...]
    rate_ref[...] = ext[pl.ds(pl.multiple_of(me * own, own), own + 8), nv:][2 : own + 6]
    courant = courant_row(me * nv, nv)
    for j in range(blocks):
        new = advect(ext[j * own : j * own + own + 8, :nv], courant)
        for h in range(nv // 128):
            out_ref[j, h * wide : (h + 1) * wide, :] = new[:, h * 128 : (h + 1) * 128]


def collide_kernel(g_ref, rate_ref, w_ref, hi_ref, lo_ref, out_ref, a_ref, l_ref, c_ref, m_ref):
    blocks = g_ref.shape[0]
    wide = g_ref.shape[1] // 2
    own = wide - 4
    nv = V // blocks
    pad = 48

    def put(columns, value, at):
        hi, lo = split(value)
        rows = value.shape[0]
        l_ref[0:rows, columns] = hi
        l_ref[at : at + rows, columns] = lo

    def correction(rows, at):
        left = l_ref[: 2 * at, :]
        both = dot(left, hi_ref[...])
        coef = both[:rows] + both[at : at + rows] + dot(left[:at], lo_ref[...])[:rows]
        hi, lo = split(coef * w_ref[...])
        m_ref[0:rows, :] = hi
        m_ref[at : at + rows, :] = lo
        right = m_ref[: 2 * at, :]
        c_ref[: 2 * at, :] = dot_t(right, hi_ref[...])
        c_ref[:at, :] += dot_t(right[:at], lo_ref[...])

    for i in range(blocks):
        for h in range(nv // 128):
            part = g_ref[i, h * wide : (h + 1) * wide, :]
            columns = slice(i * nv + h * 128, i * nv + (h + 1) * 128)
            a_ref[:wide, columns] = part
            put(columns, part, pad)
    correction(wide, pad)
    rate = rate_ref[...]
    for i in range(V // 128):
        columns = slice(i * 128, (i + 1) * 128)
        f = a_ref[:wide, columns] - rate * (c_ref[0:wide, columns] + c_ref[pad : pad + wide, columns])
        new = advect(f, courant_row(i * 128, 128))
        a_ref[:own, columns] = new
        put(columns, new, own)
    correction(own, own)
    rate = rate[2 : own + 2]
    for i in range(V // 128):
        columns = slice(i * 128, (i + 1) * 128)
        f = a_ref[:own, columns] - rate * (c_ref[0:own, columns] + c_ref[own : 2 * own, columns])
        j = i * 128 // nv
        out_ref[j, :, i * 128 - j * nv : i * 128 - j * nv + 128] = f


def unflip_kernel(t_ref, out_ref):
    out_ref[...] = t_ref[...].T


def params(mib):
    return pltpu.CompilerParams(vmem_limit_bytes=mib * 1024 * 1024)


def vmem(count):
    return [pl.BlockSpec(memory_space=pltpu.VMEM)] * count


def shards(distribution, cell_kind, type_rates, mode_weights):
    nv, nx = distribution.shape
    blocks = lax.axis_size("vel")
    slabs = lax.axis_size("space")
    own = nx // blocks
    forward = [(i, (i + 1) % slabs) for i in range(slabs)]
    backward = [(target, source) for source, target in forward]
    turned, first, last = pl.pallas_call(
        flip_kernel,
        out_shape=(
            jax.ShapeDtypeStruct((nx, nv + 128), F32),
            jax.ShapeDtypeStruct((4, nv + 128), F32),
            jax.ShapeDtypeStruct((4, nv + 128), F32),
        ),
        in_specs=[pl.BlockSpec(memory_space=pltpu.SMEM)] + vmem(2),
        out_specs=tuple(vmem(3)),
        compiler_params=params(8),
        name="flip",
    )(type_rates[None, :], distribution, cell_kind[None, :])
    low = lax.ppermute(last, "space", forward)
    high = lax.ppermute(first, "space", backward)
    fhi, flo = pl.pallas_call(
        factor_kernel,
        out_shape=(jax.ShapeDtypeStruct((V, K), BF16), jax.ShapeDtypeStruct((V, K), BF16)),
        in_specs=vmem(4),
        out_specs=tuple(vmem(2)),
        compiler_params=params(12),
        name="factors",
    )(*[jnp.asarray(t) for t in tables()])
    sent, rate = pl.pallas_call(
        functools.partial(step_kernel, blocks),
        out_shape=(
            jax.ShapeDtypeStruct((blocks, 2 * (own + 4), nv // 2), F32),
            jax.ShapeDtypeStruct((own + 4, 128), F32),
        ),
        in_specs=vmem(3),
        out_specs=tuple(vmem(2)),
        scratch_shapes=[pltpu.VMEM((nx + 8, nv + 128), F32)],
        compiler_params=params(8),
        name="transport",
    )(turned, low, high)
    got = lax.all_to_all(sent, "vel", 0, 0, tiled=True)
    back = pl.pallas_call(
        collide_kernel,
        out_shape=jax.ShapeDtypeStruct((blocks, own, nv), F32),
        in_specs=vmem(5),
        out_specs=pl.BlockSpec(memory_space=pltpu.VMEM),
        scratch_shapes=[
            pltpu.VMEM((40, V), F32),
            pltpu.VMEM((96, V), BF16),
            pltpu.VMEM((96, V), F32),
            pltpu.VMEM((96, K), BF16),
        ],
        compiler_params=params(24),
        name="collide",
    )(got, rate, mode_weights[None, :], fhi, flo)
    result = lax.all_to_all(back, "vel", 0, 0, tiled=True)
    return pl.pallas_call(
        unflip_kernel,
        out_shape=jax.ShapeDtypeStruct((nv, nx), F32),
        in_specs=vmem(1),
        out_specs=pl.BlockSpec(memory_space=pltpu.VMEM),
        compiler_params=params(8),
        name="unflip",
    )(result.reshape(nx, nv))


def solution(mesh):
    return jax.shard_map(
        shards,
        mesh=mesh,
        in_specs=(P("vel", "space"), P("space"), P(), P()),
        out_specs=P("vel", "space"),
        check_vma=False,
    )
```

time: 691 us -> 82.5 us (0.12)
  the two profiles are of different devices: /device:TPU:16 before, /device:TPU:8 now
where the time goes in v1:
time: 82.5 us; the launch traced here: 81.9 us
  starting transfers between devices  30.2 us (37%)
  blocking collectives  18.7 us (23%)
  local copies, waits for them, and re-layouts  15 us (18%)
  Pallas kernels  13.7 us (17%)
  waiting for transfers between devices  4.3 us (5%)
    all_to_all x1, blocking collectives, shards(): result = lax.all_to_all(back, 'vel', 0, 0, tiled=True)  18.7 us
    ppermute x1, starting transfers between devices, shards(): high = lax.ppermute(first, 'space', backward)  18.6 us
    unnamed x24, local copies, waits for them, and re-layouts  15 us
    all_to_all x1, starting transfers between devices, shards(): got = lax.all_to_all(sent, 'vel', 0, 0, tiled=True)  9.73 us
    pallas_call x1, Pallas kernels, shards(): pl.pallas_call(collide_kernel, out_shape=jax.ShapeDtypeStruct((blocks, ow...  8.22 us
    all_to_all x1, waiting for transfers between devices, shards(): got = lax.all_to_all(sent, 'vel', 0, 0, tiled=True)  2.98 us
    pallas_call x1, Pallas kernels, shards(): pl.pallas_call(factor_kernel, out_shape=(jax.ShapeDtypeStruct((V, K), BF1...  2.12 us
    ppermute x1, starting transfers between devices, shards(): low = lax.ppermute(last, 'space', forward)  1.92 us
  transfers between devices with their start and end apart: 3, of which 2 were waited for; matrix products, arithmetic and copies ran while one was open for 0% of the time, Pallas kernels for 3%

profile of v1, /device:TPU:8, one launch (start us, length us, event | category | flops | bytes accessed | tf_op | source)
XLA Modules:
  0.0 81.9 jit_solution(9471368512084221496)
XLA Ops:
  0.0 1.0 %copy-done.4 = f32[256,512]{1,0:T(8,128)S(1)} copy-done((f32[256,512]{1,0:T(8,128)S(1)}, f32[256,512]{1,0:T(8,128)}, u32[]{:S(2)}) %copy-start.4) | copy-done | bytes 524312
  1.0 0.7 copy-done.9
  1.7 0.7 copy-done.11
  2.4 0.8 flip.1
  3.2 1.9 %collective-permute-start = (f32[4,384]{1,0:T(4,128)S(1)}, f32[4,384]{1,0:T(4,128)S(1)}, u32[]{:S(2)}, u32[]{:S(2)}) collective-permute-start(f32[4,384]{1,0:T(4,128)S(1)} %get-tuple-element.13), channel_id=1, source_target_pairs={{0,1},{1,2},{2,3},{3,4},{4,5},{5,6},{6,7},{7,8},{8,9},{9,10},{10,1... | collective-permute-start | bytes 18440 | tf_op jit(solution)/shard_map/ppermute | solution.py:183
  5.1 18.6 %collective-permute-start.1 = (f32[4,384]{1,0:T(4,128)S(1)}, f32[4,384]{1,0:T(4,128)S(1)}, u32[]{:S(2)}, u32[]{:S(2)}) collective-permute-start(f32[4,384]{1,0:T(4,128)S(1)} %get-tuple-element.14), channel_id=1, source_target_pairs={{1,0},{2,1},{3,2},{4,3},{5,4},{6,5},{7,6},{8,7},{9,8},{10,9},{11,1... | collective-permute-start | bytes 18440 | tf_op jit(solution)/shard_map/ppermute | solution.py:184
  23.7 0.0 collective-permute-done.low_ref
  23.7 1.3 %collective-permute-done.1.high_ref = f32[4,384]{1,0:T(4,128)S(1)} collective-permute-done((f32[4,384]{1,0:T(4,128)S(1)}, f32[4,384]{1,0:T(4,128)S(1)}, u32[]{:S(2)}, u32[]{:S(2)}) %collective-permute-start.1) | collective-permute-done | bytes 6176 | tf_op jit(solution)/shard_map/ppermute | solution.py:184
  25.0 1.5 %transport.1 = (f32[16,72,128]{2,1,0:T(8,128)}, f32[36,128]{1,0:T(8,128)S(1)}) custom-call(f32[512,384]{1,0:T(8,128)S(1)} %get-tuple-element.12.t_ref, f32[4,384]{1,0:T(4,128)S(1)} %collective-permute-done.low_ref, f32[4,384]{1,0:T(4,128)S(1)} %collective-permute-done.1.high_ref), custom_call_target="tpu_custom_call" | custom-call | tf_op jit(solution)/shard_map/transport/pallas_call | solution.py:193
  26.6 9.7 %all-to-all-start = ((f32[16,72,128]{2,1,0:T(8,128)}), f32[16,72,128]{2,1,0:T(8,128)S(1)}, u32[]{:S(2)}, u32[]{:S(2)}) async-start(f32[16,72,128]{2,1,0:T(8,128)} %get-tuple-element.15), calls=%async_computation | async-start | bytes 1179648 | tf_op jit(solution)/shard_map/all_to_all | solution.py:205
  36.3 0.9 %copy-done.5 = f32[64,512]{1,0:T(8,128)S(1)} copy-done((f32[64,512]{1,0:T(8,128)S(1)}, f32[64,512]{1,0:T(8,128)}, u32[]{:S(2)}) %copy-start.5) | copy-done | bytes 131096
  37.2 0.9 %copy-done.6 = f32[64,512]{1,0:T(8,128)S(1)} copy-done((f32[64,512]{1,0:T(8,128)S(1)}, f32[64,512]{1,0:T(8,128)}, u32[]{:S(2)}) %copy-start.6) | copy-done | bytes 131096
  38.1 0.9 %copy-done.7 = f32[64,512]{1,0:T(8,128)S(1)} copy-done((f32[64,512]{1,0:T(8,128)S(1)}, f32[64,512]{1,0:T(8,128)}, u32[]{:S(2)}) %copy-start.7) | copy-done | bytes 131096
  39.0 0.9 %copy-done.8 = f32[64,512]{1,0:T(8,128)S(1)} copy-done((f32[64,512]{1,0:T(8,128)S(1)}, f32[64,512]{1,0:T(8,128)}, u32[]{:S(2)}) %copy-start.8) | copy-done | bytes 131096
  39.9 2.1 %factors.1 = (bf16[4096,512]{1,0:T(8,128)(2,1)S(1)}, bf16[4096,512]{1,0:T(8,128)(2,1)S(1)}) custom-call(f32[64,512]{1,0:T(8,128)S(1)} %copy-done.8, f32[64,512]{1,0:T(8,128)S(1)} %copy-done.7, f32[64,512]{1,0:T(8,128)S(1)} %copy-done.6, f32[64,512]{1,0:T(8,128)S(1)} %copy-done.5), custom_call_target="tpu_custom_call" | custom-call | tf_op jit(solution)/shard_map/factors/pallas_call | solution.py:185
  42.0 1.9 %copy-done = bf16[4096,512]{1,0:T(8,128)(2,1)} copy-done((bf16[4096,512]{1,0:T(8,128)(2,1)}, bf16[4096,512]{1,0:T(8,128)(2,1)S(1)}, u32[]{:S(2)}) %copy-start) | copy-done | bytes 4194328
  44.0 2.0 %copy-done.2 = bf16[4096,512]{1,0:T(8,128)(2,1)} copy-done((bf16[4096,512]{1,0:T(8,128)(2,1)}, bf16[4096,512]{1,0:T(8,128)(2,1)S(1)}, u32[]{:S(2)}) %copy-start.2) | copy-done | bytes 4194328
  46.0 3.0 %all-to-all-done.g_ref = f32[16,72,128]{2,1,0:T(8,128)S(1)} async-done(((f32[16,72,128]{2,1,0:T(8,128)}), f32[16,72,128]{2,1,0:T(8,128)S(1)}, u32[]{:S(2)}, u32[]{:S(2)}) %all-to-all-start) | async-done | bytes 589856 | tf_op jit(solution)/shard_map/all_to_all | solution.py:205
  49.0 2.2 %copy-done.1 = bf16[4096,512]{1,0:T(8,128)(2,1)S(1)} copy-done((bf16[4096,512]{1,0:T(8,128)(2,1)S(1)}, bf16[4096,512]{1,0:T(8,128)(2,1)}, u32[]{:S(2)}) %copy-start.1) | copy-done | bytes 4194328
  51.1 2.2 %copy-done.3 = bf16[4096,512]{1,0:T(8,128)(2,1)S(1)} copy-done((bf16[4096,512]{1,0:T(8,128)(2,1)S(1)}, bf16[4096,512]{1,0:T(8,128)(2,1)}, u32[]{:S(2)}) %copy-start.3) | copy-done | bytes 4194328
  53.3 0.7 copy-done.10
  54.0 8.2 %collide.1 = f32[16,32,256]{2,1,0:T(8,128)S(1)} custom-call(f32[16,72,128]{2,1,0:T(8,128)S(1)} %all-to-all-done.g_ref, f32[36,128]{1,0:T(8,128)S(1)} %get-tuple-element.16.rate_ref, f32[1,512]{1,0:T(1,128)S(1)} %bitcast.6, bf16[4096,512]{1,0:T(8,128)(2,1)S(1)} %copy-done.1, bf16[4096,512]{1,0:T(8,128)(2,1)S(1)} %copy-done.3), custom_call_target="tpu_custom_call" | custom-call | tf_op jit(solution)/shard_map/collide/pallas_call | solution.py:206
  62.2 18.7 %all_to_all.10 = f32[16,32,256]{2,1,0:T(8,128)S(1)} all-to-all(f32[16,32,256]{2,1,0:T(8,128)S(1)} %collide.1), channel_id=1, replica_groups=mesh['vel'=16,'space'=64] {'vel'}, dimensions={0} | all-to-all | bytes 1048576 | tf_op jit(solution)/shard_map/all_to_all | solution.py:220
  80.9 1.0 %unflip.1 = f32[256,512]{1,0:T(8,128)} custom-call(f32[512,256]{1,0:T(8,128)S(1)} %bitcast.4), custom_call_target="tpu_custom_call" | custom-call | tf_op jit(solution)/shard_map/unflip/pallas_call | solution.py:221
  (12 shorter events, 0.0 us)
Async XLA Ops:
  0.0 1.0 %copy-start.4 = (f32[256,512]{1,0:T(8,128)S(1)}, f32[256,512]{1,0:T(8,128)}, u32[]{:S(2)}) copy-start(f32[256,512]{1,0:T(8,128)} %f_ref.1) | copy-start | bytes 1572868
  1.0 0.7 copy-start.9
  1.7 0.7 copy-start.11
  3.2 20.5 %collective-permute-start = (f32[4,384]{1,0:T(4,128)S(1)}, f32[4,384]{1,0:T(4,128)S(1)}, u32[]{:S(2)}, u32[]{:S(2)}) collective-permute-start(f32[4,384]{1,0:T(4,128)S(1)} %get-tuple-element.13), channel_id=1, source_target_pairs={{0,1},{1,2},{2,3},{3,4},{4,5},{5,6},{6,7},{7,8},{8,9},{9,10},{10,1... | collective-permute-start | bytes 18440 | tf_op jit(solution)/shard_map/ppermute | solution.py:183
  5.1 19.9 %collective-permute-start.1 = (f32[4,384]{1,0:T(4,128)S(1)}, f32[4,384]{1,0:T(4,128)S(1)}, u32[]{:S(2)}, u32[]{:S(2)}) collective-permute-start(f32[4,384]{1,0:T(4,128)S(1)} %get-tuple-element.14), channel_id=1, source_target_pairs={{1,0},{2,1},{3,2},{4,3},{5,4},{6,5},{7,6},{8,7},{9,8},{10,9},{11,1... | collective-permute-start | bytes 18440 | tf_op jit(solution)/shard_map/ppermute | solution.py:184
  26.6 22.4 %all-to-all-start = ((f32[16,72,128]{2,1,0:T(8,128)}), f32[16,72,128]{2,1,0:T(8,128)S(1)}, u32[]{:S(2)}, u32[]{:S(2)}) async-start(f32[16,72,128]{2,1,0:T(8,128)} %get-tuple-element.15), calls=%async_computation | async-start | bytes 1179648 | tf_op jit(solution)/shard_map/all_to_all | solution.py:205
  36.3 0.9 %copy-start.5 = (f32[64,512]{1,0:T(8,128)S(1)}, f32[64,512]{1,0:T(8,128)}, u32[]{:S(2)}) copy-start(f32[64,512]{1,0:T(8,128)} %constant.11.clone.cs_ref) | copy-start | bytes 393220
  37.2 0.9 %copy-start.6 = (f32[64,512]{1,0:T(8,128)S(1)}, f32[64,512]{1,0:T(8,128)}, u32[]{:S(2)}) copy-start(f32[64,512]{1,0:T(8,128)} %constant.10.clone.cc_ref) | copy-start | bytes 393220
  38.1 0.9 %copy-start.7 = (f32[64,512]{1,0:T(8,128)S(1)}, f32[64,512]{1,0:T(8,128)}, u32[]{:S(2)}) copy-start(f32[64,512]{1,0:T(8,128)} %constant.9.clone.fs_ref) | copy-start | bytes 393220
  39.0 0.9 %copy-start.8 = (f32[64,512]{1,0:T(8,128)S(1)}, f32[64,512]{1,0:T(8,128)}, u32[]{:S(2)}) copy-start(f32[64,512]{1,0:T(8,128)} %constant.8.clone.fc_ref) | copy-start | bytes 393220
  42.0 2.0 %copy-start = (bf16[4096,512]{1,0:T(8,128)(2,1)}, bf16[4096,512]{1,0:T(8,128)(2,1)S(1)}, u32[]{:S(2)}) copy-start(bf16[4096,512]{1,0:T(8,128)(2,1)S(1)} %get-tuple-element.17.hi_ref) | copy-start | bytes 12582916
  44.0 2.0 %copy-start.2 = (bf16[4096,512]{1,0:T(8,128)(2,1)}, bf16[4096,512]{1,0:T(8,128)(2,1)S(1)}, u32[]{:S(2)}) copy-start(bf16[4096,512]{1,0:T(8,128)(2,1)S(1)} %get-tuple-element.18.lo_ref) | copy-start | bytes 12582916
  49.0 2.2 %copy-start.1 = (bf16[4096,512]{1,0:T(8,128)(2,1)S(1)}, bf16[4096,512]{1,0:T(8,128)(2,1)}, u32[]{:S(2)}) copy-start(bf16[4096,512]{1,0:T(8,128)(2,1)} %copy-done) | copy-start | bytes 12582916
  51.1 2.2 %copy-start.3 = (bf16[4096,512]{1,0:T(8,128)(2,1)S(1)}, bf16[4096,512]{1,0:T(8,128)(2,1)}, u32[]{:S(2)}) copy-start(bf16[4096,512]{1,0:T(8,128)(2,1)} %copy-done.2) | copy-start | bytes 12582916
  53.3 0.7 copy-start.10

commit v2 on v1

v2 whole, which is shorter than its diff:
```python
import functools
import math

import jax
import jax.numpy as jnp
import numpy as np
from jax import lax
from jax.experimental import pallas as pl
from jax.experimental.pallas import tpu as pltpu
from jax.sharding import PartitionSpec as P

V = 4096
K = 512
H = V // 2
B = 64
A = H // B
LANES = 256
courant_limit = 0.9
F32 = jnp.float32
BF16 = jnp.bfloat16


def tables():
    k = np.concatenate([np.arange(0, K, 2), np.arange(1, K, 2)])
    scale = np.where(k == 0, math.sqrt(1.0 / V), math.sqrt(2.0 / V))
    fine = (2 * np.arange(B) + 1)[:, None] * k[None, :] % (4 * V) * (math.pi / (2 * V))
    coarse = (2 * B * np.arange(A))[:, None] * k[None, :] % (4 * V) * (math.pi / (2 * V))
    parts = (np.cos(fine) * scale, np.sin(fine) * scale, np.cos(coarse), np.sin(coarse))
    return np.concatenate(parts).astype(np.float32)


def window_of(rank, blocks):
    return [0, blocks - 1][rank] if rank < 2 else rank - 1


def split(x):
    hi = x.astype(BF16)
    return hi, (x - hi.astype(F32)).astype(BF16)


def dot(a, b):
    return lax.dot_general(a, b, (((1,), (0,)), ((), ())), preferred_element_type=F32)


def dot_t(a, b):
    return lax.dot_general(a, b, (((1,), (1,)), ((), ())), preferred_element_type=F32)


def exact_dot(x, picks):
    hi = x.astype(BF16)
    rest = x - hi.astype(F32)
    mid = rest.astype(BF16)
    low = (rest - mid.astype(F32)).astype(BF16)
    return dot(hi, picks) + (dot(mid, picks) + dot(low, picks))


def minmod(a, b):
    zero = jnp.zeros_like(a)
    return jnp.minimum(jnp.maximum(a, zero), jnp.maximum(b, zero)) + jnp.maximum(
        jnp.minimum(a, zero), jnp.minimum(b, zero)
    )


def advect(padded, courant, positive):
    width = padded.shape[0] - 4
    differences = padded[1:] - padded[:-1]
    slopes = minmod(differences[:-1], differences[1:])
    if positive:
        face = padded[1 : width + 2] + 0.5 * (1.0 - courant) * slopes[0 : width + 1]
    else:
        face = padded[2 : width + 3] - 0.5 * (1.0 + courant) * slopes[1 : width + 2]
    return padded[2 : width + 2] - courant * (face[1:] - face[:-1])


def courant_row(velocity):
    return (2 * velocity + 1 - V).astype(F32) * (courant_limit / V)


def flip_kernel(blocks, rates_ref, kind_ref, f_hbm, out_ref, rate_ref, f_ref, ext, rates_ext, sems):
    me = lax.axis_index("vel")
    nv, nx = f_ref.shape
    own = nx // blocks
    parts = nx // 128
    copies = [
        pltpu.make_async_copy(
            f_hbm.at[:, p * 128 : (p + 1) * 128], f_ref.at[:, p * 128 : (p + 1) * 128], sems.at[p]
        )
        for p in range(parts)
    ]
    for copy in copies:
        copy.start()
    kinds = kind_ref[...]
    rate = jnp.zeros(kinds.shape, F32)
    for j in range(rates_ref.shape[1]):
        rate = jnp.where(kinds == j, rates_ref[0, j], rate)
    rates_ext[8 : nx + 8, :] = jnp.broadcast_to(rate, (128, nx)).T
    rates_ext[0:8, :] = jnp.zeros((8, 128), F32)
    rates_ext[nx + 8 :, :] = jnp.zeros((8, 128), F32)
    spot = jnp.where(me == 0, 0, jnp.where(me == 1, blocks - 1, me - 1))
    rate_ref[...] = rates_ext[pl.ds(pl.multiple_of(spot * own, own), own + 16), :][4 : own + 12]
    for p in range(parts):
        copies[p].wait()
        ext[8 + p * 128 : 8 + (p + 1) * 128, :] = f_ref[:, p * 128 : (p + 1) * 128].T
    first = rates_ext[8:12, :]
    last = rates_ext[nx + 4 : nx + 8, :]
    for h in range(nv // 128):
        ext[4:8, h * 128 : (h + 1) * 128] = first
        ext[nx + 8 : nx + 12, h * 128 : (h + 1) * 128] = last
    for r in range(blocks):
        at = 4 + window_of(r, blocks) * own
        out_ref[r] = ext[at : at + own + 8, :]


def factor_kernel(table_hbm, w_ref, edge_hbm, hi_ref, lo_ref, wp_ref, table, sem):
    copy = pltpu.make_async_copy(table_hbm, table, sem)
    copy.start()
    source = lax.broadcasted_iota(jnp.int32, (K, K), 0)
    target = lax.broadcasted_iota(jnp.int32, (K, K), 1)
    mode = jnp.where(target < K // 2, 2 * target, 2 * target + 1 - K)
    picks = jnp.where(source == mode, 1.0, 0.0).astype(BF16)
    wp_ref[...] = exact_dot(jnp.broadcast_to(w_ref[...], (8, K)), picks)
    copy.wait()

    def body(a, carry):
        f = table[0:B, :] * table[pl.ds(2 * B + a, 1), :] - table[B : 2 * B, :] * table[pl.ds(2 * B + A + a, 1), :]
        hi, lo = split(f)
        rows = pl.ds(pl.multiple_of(a * B, B), B)
        hi_ref[rows, :] = hi
        lo_ref[rows, :] = lo
        return carry

    lax.fori_loop(0, A, body, 0)


def collide_kernel(g_ref, e_ref, rate_in, wp_ref, hi_ref, lo_ref, out_ref, a_ref, b_ref, r_ref, l_ref, c_ref, m_ref):
    me = lax.axis_index("vel")
    blocks, window, nv = g_ref.shape
    own = window - 8
    wide = window - 4
    pad = 48
    half = K // 2
    lower = [slice(c * LANES, (c + 1) * LANES) for c in range(H // LANES)]
    upper = [slice(H + c * LANES, H + (c + 1) * LANES) for c in range(H // LANES)]
    lane = lax.broadcasted_iota(jnp.int32, (1, LANES), 1)
    turn = jnp.where(
        lax.broadcasted_iota(jnp.int32, (LANES, LANES), 0)
        + lax.broadcasted_iota(jnp.int32, (LANES, LANES), 1)
        == LANES - 1,
        1.0,
        0.0,
    ).astype(BF16)

    for i in range(blocks):
        a_ref[:, i * nv : (i + 1) * nv] = g_ref[i]
    r_ref[...] = rate_in[...]

    @pl.when(me == 0)
    def _():
        for i in range(blocks):
            a_ref[0:4, i * nv : (i + 1) * nv] = e_ref[i, 0:4, :]
        r_ref[0:4, :] = e_ref[0, 4:8, :128]

    @pl.when(me == 1)
    def _():
        for i in range(blocks):
            a_ref[window - 4 :, i * nv : (i + 1) * nv] = e_ref[i, 4:8, :]
        r_ref[window - 4 :, :] = e_ref[0, 0:4, :128]

    def fold(c, up, down, at):
        rows = up.shape[0]
        for part, columns in ((up + down, lower[c]), (up - down, upper[c])):
            hi, lo = split(part)
            l_ref[0:rows, columns] = hi
            l_ref[at : at + rows, columns] = lo

    def correction(rows, at):
        for s in range(2):
            modes = slice(s * half, (s + 1) * half)
            left = l_ref[: 2 * at, s * H : (s + 1) * H]
            both = dot(left, hi_ref[:, modes])
            coef = both[:rows] + both[at : at + rows] + dot(left[:at], lo_ref[:, modes])[:rows]
            hi, lo = split(coef * wp_ref[0:1, modes])
            m_ref[0:rows, modes] = hi
            m_ref[at : at + rows, modes] = lo
            right = m_ref[: 2 * at, modes]
            back = dot_t(right, hi_ref[:, modes])
            c_ref[:rows, s * H : (s + 1) * H] = (
                back[:rows] + back[at : at + rows] + dot_t(right[:at], lo_ref[:, modes])[:rows]
            )

    def courants(c):
        v = lane + c * LANES
        return courant_row(v), courant_row(V - 1 - v)

    def mirror(c):
        return slice(V - (c + 1) * LANES, V - c * LANES)

    for c in range(H // LANES):
        down, up = courants(c)
        new = advect(a_ref[:, lower[c]], down, False)
        turned = advect(exact_dot(a_ref[:, mirror(c)], turn), up, True)
        b_ref[:wide, lower[c]] = new
        b_ref[:wide, upper[c]] = turned
        fold(c, new, turned, pad)
    correction(wide, pad)
    rate = jnp.concatenate([r_ref[2 : wide + 2, :]] * (LANES // 128), axis=1)
    for c in range(H // LANES):
        down, up = courants(c)
        even, odd = c_ref[:wide, lower[c]], c_ref[:wide, upper[c]]
        new = advect(b_ref[:wide, lower[c]] - rate * (even + odd), down, False)
        turned = advect(b_ref[:wide, upper[c]] - rate * (even - odd), up, True)
        b_ref[:own, lower[c]] = new
        b_ref[:own, upper[c]] = turned
        fold(c, new, turned, own)
    correction(own, own)
    rate = rate[2 : own + 2]
    for c in range(H // LANES):
        even, odd = c_ref[:own, lower[c]], c_ref[:own, upper[c]]
        out_ref[c] = b_ref[:own, lower[c]] - rate * (even + odd)
        out_ref[blocks - 1 - c] = exact_dot(b_ref[:own, upper[c]] - rate * (even - odd), turn)


def unflip_kernel(t_ref, out_ref):
    blocks, own, _ = t_ref.shape
    order = sorted(range(blocks), key=lambda r: window_of(r, blocks))
    per = 128 // own
    for p in range(blocks // per):
        rows = jnp.concatenate([t_ref[r] for r in order[p * per : (p + 1) * per]], axis=0)
        out_ref[:, p * 128 : (p + 1) * 128] = rows.T


def params(mib):
    return pltpu.CompilerParams(vmem_limit_bytes=mib * 1024 * 1024)


VMEM = pl.BlockSpec(memory_space=pltpu.VMEM)
SMEM = pl.BlockSpec(memory_space=pltpu.SMEM)
ANY = pl.BlockSpec(memory_space=pl.ANY)


def shards(distribution, cell_kind, type_rates, mode_weights):
    nv, nx = distribution.shape
    blocks = lax.axis_size("vel")
    slabs = lax.axis_size("space")
    own = nx // blocks
    window = own + 8
    sent, rate = pl.pallas_call(
        functools.partial(flip_kernel, blocks),
        out_shape=(
            jax.ShapeDtypeStruct((blocks, window, nv), F32),
            jax.ShapeDtypeStruct((window, 128), F32),
        ),
        in_specs=[SMEM, VMEM, ANY],
        out_specs=(VMEM, VMEM),
        scratch_shapes=[
            pltpu.VMEM((nv, nx), F32),
            pltpu.VMEM((nx + 16, nv), F32),
            pltpu.VMEM((nx + 16, 128), F32),
            pltpu.SemaphoreType.DMA((nx // 128,)),
        ],
        compiler_params=params(8),
        name="flip",
    )(type_rates[None, :], cell_kind[None, :], distribution)
    got = lax.all_to_all(sent, "vel", 0, 0, tiled=True)
    me = lax.axis_index("vel")
    edge = lax.dynamic_slice_in_dim(got, jnp.where(me == 0, 0, window - 8), 8, axis=1)
    pairs = []
    for s in range(slabs):
        after = (s + 1) % slabs
        pairs += [(slabs + s, after), (after, slabs + s)]
    edge_in = lax.ppermute(edge, ("vel", "space"), pairs)
    hi, lo, weights = pl.pallas_call(
        factor_kernel,
        out_shape=(
            jax.ShapeDtypeStruct((H, K), BF16),
            jax.ShapeDtypeStruct((H, K), BF16),
            jax.ShapeDtypeStruct((8, K), F32),
        ),
        in_specs=[ANY, VMEM, ANY],
        out_specs=(VMEM, VMEM, VMEM),
        scratch_shapes=[pltpu.VMEM((2 * (A + B), K), F32), pltpu.SemaphoreType.DMA],
        compiler_params=params(12),
        name="factors",
    )(jnp.asarray(tables()), mode_weights[None, :], edge)
    back = pl.pallas_call(
        collide_kernel,
        out_shape=jax.ShapeDtypeStruct((blocks, own, nv), F32),
        in_specs=[VMEM] * 6,
        out_specs=VMEM,
        scratch_shapes=[
            pltpu.VMEM((window, V), F32),
            pltpu.VMEM((window, V), F32),
            pltpu.VMEM((window, 128), F32),
            pltpu.VMEM((96, V), BF16),
            pltpu.VMEM((window, V), F32),
            pltpu.VMEM((96, K), BF16),
        ],
        compiler_params=params(24),
        name="collide",
    )(got, edge_in, rate, weights, hi, lo)
    result = lax.all_to_all(back, "vel", 0, 0, tiled=True)
    return pl.pallas_call(
        unflip_kernel,
        out_shape=jax.ShapeDtypeStruct((nv, nx), F32),
        in_specs=[VMEM],
        out_specs=VMEM,
        compiler_params=params(8),
        name="unflip",
    )(result)


def solution(mesh):
    return jax.shard_map(
        shards,
        mesh=mesh,
        in_specs=(P("vel", "space"), P("space"), P(), P()),
        out_specs=P("vel", "space"),
        check_vma=False,
    )
```

time: 82.5 us -> 76 us (0.921)
  waiting for transfers between devices: 4.3 us -> 17.3 us
  local copies, waits for them, and re-layouts: 15 us -> 2.41 us
  starting transfers between devices: 30.2 us -> 18.4 us
  blocking collectives: 18.7 us -> 26.7 us
  Pallas kernels: 13.7 us -> 10.8 us
    ppermute x2 -> x1, starting transfers between devices: 20.5 us -> 1.92 us  [shards(): edge_in = lax.ppermute(edge, ('vel', 'space'), pairs)]
    unnamed x24 -> x10, local copies, waits for them, and re-layouts: 15 us -> 2.4 us
    all_to_all x1, waiting for transfers between devices: 2.98 us -> 13.1 us  [shards(): got = lax.all_to_all(sent, 'vel', 0, 0, tiled=True)]
    all_to_all x1, blocking collectives: 18.7 us -> 26.7 us  [shards(): result = lax.all_to_all(back, 'vel', 0, 0, tiled=True)]
    all_to_all x1, starting transfers between devices: 9.73 us -> 16.5 us  [shards(): got = lax.all_to_all(sent, 'vel', 0, 0, tiled=True)]
    ppermute x2 -> x1, waiting for transfers between devices: 1.32 us -> 4.14 us  [shards(): edge_in = lax.ppermute(edge, ('vel', 'space'), pairs)]
    pallas_call x1, Pallas kernels: 8.22 us -> 6.2 us  [shards(): pl.pallas_call(collide_kernel, out_shape=jax.ShapeDtypeStruct((blocks, ow...]
    pallas_call x3 -> x2, Pallas kernels: 4.44 us -> 3.65 us  [the longest x1 2.05 us: shards(): pl.pallas_call(functools.partial(flip_kernel, blocks), out_shape=(jax.Sha...]
  transfers between devices with their start and end apart: 3 -> 2, of which waited for: 2 -> 2; matrix products, arithmetic and copies ran while one was open for 0% -> 0% of each run, Pallas kernels for 3% -> 2%
where the time goes in v2:
time: 76 us; the launch traced here: 75.7 us
  blocking collectives  26.7 us (35%)
  starting transfers between devices  18.4 us (24%)
  waiting for transfers between devices  17.3 us (23%)
  Pallas kernels  10.8 us (14%)
  local copies, waits for them, and re-layouts  2.41 us (3%)
    all_to_all x1, blocking collectives, shards(): result = lax.all_to_all(back, 'vel', 0, 0, tiled=True)  26.7 us
    all_to_all x1, starting transfers between devices, shards(): got = lax.all_to_all(sent, 'vel', 0, 0, tiled=True)  16.5 us
    all_to_all x1, waiting for transfers between devices, shards(): got = lax.all_to_all(sent, 'vel', 0, 0, tiled=True)  13.1 us
    pallas_call x1, Pallas kernels, shards(): pl.pallas_call(collide_kernel, out_shape=jax.ShapeDtypeStruct((blocks, ow...  6.2 us
    ppermute x1, waiting for transfers between devices, shards(): edge_in = lax.ppermute(edge, ('vel', 'space'), pairs)  4.14 us
    unnamed x10, local copies, waits for them, and re-layouts  2.4 us
    pallas_call x1, Pallas kernels, shards(): pl.pallas_call(functools.partial(flip_kernel, blocks), out_shape=(jax.Sha...  2.05 us
    ppermute x1, starting transfers between devices, shards(): edge_in = lax.ppermute(edge, ('vel', 'space'), pairs)  1.92 us
  transfers between devices with their start and end apart: 2, of which 2 were waited for; matrix products, arithmetic and copies ran while one was open for 0% of the time, Pallas kernels for 2%

profile of v2, /device:TPU:8, one launch (start us, length us, event | category | flops | bytes accessed | tf_op | source)
XLA Modules:
  0.0 75.7 jit_solution(3339689537809068504)
XLA Ops:
  0.0 0.0 copy-start.3
  0.0 0.0 copy-start
  0.0 1.1 %copy-done = f32[256,512]{1,0:T(8,128)S(1)} copy-done((f32[256,512]{1,0:T(8,128)S(1)}, f32[256,512]{1,0:T(8,128)}, u32[]{:S(2)}) %copy-start) | copy-done | bytes 524312
  1.1 0.0 copy-start.2
  1.1 0.7 copy-done.2
  1.7 0.0 copy-start.4
  1.7 0.7 copy-done.4
  2.4 0.0 copy-start.1
  2.4 2.1 %flip.1 = (f32[16,40,256]{2,1,0:T(8,128)}, f32[40,128]{1,0:T(8,128)S(1)}) custom-call(f32[1,4]{1,0:T(1,128)S(1)} %bitcast.5, s32[1,512]{1,0:T(1,128)S(1)} %bitcast.3, f32[256,512]{1,0:T(8,128)S(1)} %copy-done), custom_call_target="tpu_custom_call" | custom-call | tf_op jit(solution)/shard_map/flip/pallas_call | solution.py:247
  4.5 16.5 %all-to-all-start = ((f32[16,40,256]{2,1,0:T(8,128)}), f32[16,40,256]{2,1,0:T(8,128)S(1)}, u32[]{:S(2)}, u32[]{:S(2)}) async-start(f32[16,40,256]{2,1,0:T(8,128)} %get-tuple-element.10), calls=%async_computation | async-start | bytes 1310720 | tf_op jit(solution)/shard_map/all_to_all | solution.py:264
  20.9 13.1 %all-to-all-done.g_ref = f32[16,40,256]{2,1,0:T(8,128)S(1)} async-done(((f32[16,40,256]{2,1,0:T(8,128)}), f32[16,40,256]{2,1,0:T(8,128)S(1)}, u32[]{:S(2)}, u32[]{:S(2)}) %all-to-all-start) | async-done | bytes 655392 | tf_op jit(solution)/shard_map/all_to_all | solution.py:264
  34.1 1.9 %collective-permute-start = (f32[16,8,256]{2,1,0:T(8,128)S(1)}, f32[16,8,256]{2,1,0:T(8,128)S(1)}, u32[]{:S(2)}, u32[]{:S(2)}) collective-permute-start(f32[16,8,256]{2,1,0:T(8,128)S(1)} %constant_dynamic-slice_fusion.edge_hbm), channel_id=1, source_target_pairs={{64,1},{1,64},{65,2},{2,65},{66,3},{3,66},{67,4},{4,67},{68,5},{5,... | collective-permute-start | bytes 393224 | tf_op jit(solution)/shard_map/ppermute | solution.py:271
  36.0 0.0 copy-done.3
  36.0 0.0 copy-done.1
  36.0 1.6 %factors.1 = (bf16[2048,512]{1,0:T(8,128)(2,1)S(1)}, bf16[2048,512]{1,0:T(8,128)(2,1)S(1)}, f32[8,512]{1,0:T(8,128)S(1)}) custom-call(f32[192,512]{1,0:T(8,128)S(1)} %copy-done.1, f32[1,512]{1,0:T(1,128)S(1)} %bitcast.4, f32[16,8,256]{2,1,0:T(8,128)S(1)} %constant_dynamic-slice_fusion.edge_hbm), custom_call_target="tpu_custom_call" | custom-call | tf_op jit(solution)/shard_map/factors/pallas_call | solution.py:272
  37.6 4.1 %collective-permute-done.e_ref = f32[16,8,256]{2,1,0:T(8,128)S(1)} collective-permute-done((f32[16,8,256]{2,1,0:T(8,128)S(1)}, f32[16,8,256]{2,1,0:T(8,128)S(1)}, u32[]{:S(2)}, u32[]{:S(2)}) %collective-permute-start) | collective-permute-done | bytes 131104 | tf_op jit(solution)/shard_map/ppermute | solution.py:271
  41.8 6.2 %collide.1 = f32[16,32,256]{2,1,0:T(8,128)S(1)} custom-call(f32[16,40,256]{2,1,0:T(8,128)S(1)} %all-to-all-done.g_ref, f32[16,8,256]{2,1,0:T(8,128)S(1)} %collective-permute-done.e_ref, f32[40,128]{1,0:T(8,128)S(1)} %get-tuple-element.11.rate_in, f32[8,512]{1,0:T(8,128)S(1)} %get-tuple-element.12.wp_ref, bf16[2048,512]{1,0:T(8,128)(2,1)S(1)} %get-tuple-element.13.hi_ref, ...), custom_call_target="tpu_custom_call" | custom-call | tf_op jit(solution)/shard_map/collide/pallas_call | solution.py:285
  48.0 26.7 %all_to_all.10.t_ref = f32[16,32,256]{2,1,0:T(8,128)S(1)} all-to-all(f32[16,32,256]{2,1,0:T(8,128)S(1)} %collide.1), channel_id=1, replica_groups=mesh['vel'=16,'space'=64] {'vel'}, dimensions={0} | all-to-all | bytes 1048576 | tf_op jit(solution)/shard_map/all_to_all | solution.py:301
  74.7 1.0 %unflip.1 = f32[256,512]{1,0:T(8,128)} custom-call(f32[16,32,256]{2,1,0:T(8,128)S(1)} %all_to_all.10.t_ref), custom_call_target="tpu_custom_call" | custom-call | tf_op jit(solution)/shard_map/unflip/pallas_call | solution.py:302
  (1 shorter events, 0.0 us)
Async XLA Ops:
  0.0 36.0 %copy-start.3 = (f32[512]{0:T(512)S(1)}, f32[512]{0:T(512)}, u32[]{:S(2)}) copy-start(f32[512]{0:T(512)} %param.8) | copy-start | bytes 6148
  0.0 1.1 %copy-start = (f32[256,512]{1,0:T(8,128)S(1)}, f32[256,512]{1,0:T(8,128)}, u32[]{:S(2)}) copy-start(f32[256,512]{1,0:T(8,128)} %f_hbm.1) | copy-start | bytes 1572868
  1.1 0.7 copy-start.2
  1.7 0.7 copy-start.4
  2.4 33.6 %copy-start.1 = (f32[192,512]{1,0:T(8,128)S(1)}, f32[192,512]{1,0:T(8,128)}, u32[]{:S(2)}) copy-start(f32[192,512]{1,0:T(8,128)} %constant.14.clone.table_hbm) | copy-start | bytes 1179652
  4.5 29.6 %all-to-all-start = ((f32[16,40,256]{2,1,0:T(8,128)}), f32[16,40,256]{2,1,0:T(8,128)S(1)}, u32[]{:S(2)}, u32[]{:S(2)}) async-start(f32[16,40,256]{2,1,0:T(8,128)} %get-tuple-element.10), calls=%async_computation | async-start | bytes 1310720 | tf_op jit(solution)/shard_map/all_to_all | solution.py:264
  34.1 7.7 %collective-permute-start = (f32[16,8,256]{2,1,0:T(8,128)S(1)}, f32[16,8,256]{2,1,0:T(8,128)S(1)}, u32[]{:S(2)}, u32[]{:S(2)}) collective-permute-start(f32[16,8,256]{2,1,0:T(8,128)S(1)} %constant_dynamic-slice_fusion.edge_hbm), channel_id=1, source_target_pairs={{64,1},{1,64},{65,2},{2,65},{66,3},{3,66},{67,4},{4,67},{68,5},{5,... | collective-permute-start | bytes 393224 | tf_op jit(solution)/shard_map/ppermute | solution.py:271

commit v3 on v2

v3 whole, which is shorter than its diff:
```python
import functools
import math

import jax
import jax.numpy as jnp
import numpy as np
from jax import lax
from jax.experimental import pallas as pl
from jax.experimental.pallas import tpu as pltpu
from jax.sharding import PartitionSpec as P

V = 4096
K = 512
H = V // 2
B = 64
A = H // B
courant_limit = 0.9
F32 = jnp.float32
BF16 = jnp.bfloat16


def tables():
    k = np.concatenate([np.arange(0, K, 2), np.arange(1, K, 2)])
    scale = np.where(k == 0, math.sqrt(1.0 / V), math.sqrt(2.0 / V))
    fine = (2 * np.arange(B) + 1)[:, None] * k[None, :] % (4 * V) * (math.pi / (2 * V))
    coarse = (2 * B * np.arange(A))[:, None] * k[None, :] % (4 * V) * (math.pi / (2 * V))
    parts = (np.cos(fine) * scale, np.sin(fine) * scale, np.cos(coarse), np.sin(coarse))
    return np.concatenate(parts).astype(np.float32)


def split(x):
    hi = x.astype(BF16)
    return hi, (x - hi.astype(F32)).astype(BF16)


def dot(a, b):
    return lax.dot_general(a, b, (((1,), (0,)), ((), ())), preferred_element_type=F32)


def dot_t(a, b):
    return lax.dot_general(a, b, (((1,), (1,)), ((), ())), preferred_element_type=F32)


def exact_dot(x, picks):
    hi = x.astype(BF16)
    rest = x - hi.astype(F32)
    mid = rest.astype(BF16)
    low = (rest - mid.astype(F32)).astype(BF16)
    return dot(hi, picks) + (dot(mid, picks) + dot(low, picks))


def minmod(a, b):
    zero = jnp.zeros_like(a)
    return jnp.minimum(jnp.maximum(a, zero), jnp.maximum(b, zero)) + jnp.maximum(
        jnp.minimum(a, zero), jnp.minimum(b, zero)
    )


def upwind(far, near, here, other, speed):
    first = near - far
    second = here - near
    change = minmod(second, other - here) - minmod(first, second)
    return here - speed * (second + 0.5 * (1.0 - speed) * change)


def advect(at, speed, positive):
    if positive:
        return upwind(at(-2), at(-1), at(0), at(1), speed)
    return upwind(at(2), at(1), at(0), at(-1), speed)


def courant_row(velocity):
    return (2 * velocity + 1 - V).astype(F32) * (courant_limit / V)


def mirrored(x):
    lane = lax.broadcasted_iota(jnp.int32, x.shape, 1)
    return jnp.take_along_axis(x, 127 - lane, axis=1)


def place(blocks):
    me = lax.axis_index("vel")
    odd = lax.rem(lax.axis_index("space"), 2)
    return jnp.where(me > 1, me - 1, jnp.where(me == odd, 0, blocks - 1))


def flip_kernel(blocks, f_hbm, out_ref, f_ref, ext, sems):
    me = lax.axis_index("vel")
    odd = lax.rem(lax.axis_index("space"), 2)
    nv, nx = f_ref.shape
    own = nx // blocks
    wide = own + 4
    parts = nx // 128
    copies = [
        pltpu.make_async_copy(
            f_hbm.at[:, p * 128 : (p + 1) * 128], f_ref.at[:, p * 128 : (p + 1) * 128], sems.at[p]
        )
        for p in range(parts)
    ]
    for copy in copies:
        copy.start()
    lane = lax.broadcasted_iota(jnp.int32, (1, 128), 1)
    ahead = me >= blocks // 2
    speeds = [jnp.abs(courant_row(me * nv + h * 128 + lane)) for h in range(nv // 128)]

    def make(p, r):
        for h in range(nv // 128):
            base = 8 + p * own - 2

            def at(k, base=base, h=h):
                return ext[h, base + k : base + k + wide, :]

            below, above = at(-1), at(1)
            near = jnp.where(ahead, below, above)
            other = jnp.where(ahead, above, below)
            far = jnp.where(ahead, at(-2), at(2))
            out_ref[r, h * wide : (h + 1) * wide, :] = upwind(far, near, at(0), other, speeds[h])
            if p == 0:
                out_ref[r, h * wide : h * wide + 4, :] = ext[h, 8:12, :]
            if p == blocks - 1:
                out_ref[r, h * wide + own : (h + 1) * wide, :] = ext[h, nx + 4 : nx + 8, :]

    done = 0
    for p in range(parts):
        copies[p].wait()
        for h in range(nv // 128):
            ext[h, 8 + p * 128 : 8 + (p + 1) * 128, :] = f_ref[
                h * 128 : (h + 1) * 128, p * 128 : (p + 1) * 128
            ].T
        while done < blocks and (done == 0 or (done + 1) * own + 4 <= (p + 1) * 128 or p == parts - 1):
            make(done, odd if done == 0 else 1 - odd if done == blocks - 1 else done + 1)
            done += 1


def rate_kernel(blocks, rates_ref, kind_ref, rate_ref, edge_ref, ext):
    nx = kind_ref.shape[1]
    own = nx // blocks
    kinds = kind_ref[...]
    rate = jnp.zeros(kinds.shape, F32)
    for j in range(rates_ref.shape[1]):
        rate = jnp.where(kinds == j, rates_ref[0, j], rate)
    ext[0:8, :] = jnp.zeros((8, 128), F32)
    ext[8 : nx + 8, :] = jnp.broadcast_to(rate, (128, nx)).T
    ext[nx + 8 :, :] = jnp.zeros((8, 128), F32)
    spot = place(blocks)
    rate_ref[...] = ext[pl.ds(pl.multiple_of(spot * own, own), own + 16), :][6 : own + 10]
    edge_ref[...] = jnp.where(spot == 0, ext[8:16, :], ext[nx + 4 : nx + 12, :])


def edge_kernel(g_ref, rate_ref, out_ref):
    blocks, rows, _ = g_ref.shape
    wide = rows // 2
    first = place(blocks) == 0
    for i in range(blocks):
        for h in range(2):
            n = 8 * i + 4 * h
            out_ref[n : n + 4, :] = jnp.where(
                first,
                g_ref[i, h * wide : h * wide + 4, :],
                g_ref[i, (h + 1) * wide - 4 : (h + 1) * wide, :],
            )
    out_ref[8 * blocks :, :] = rate_ref[...]


def factor_kernel(table_hbm, w_ref, edge_hbm, hi_ref, lo_ref, wp_ref, table, sem):
    copy = pltpu.make_async_copy(table_hbm, table, sem)
    copy.start()
    source = lax.broadcasted_iota(jnp.int32, (K, K), 0)
    target = lax.broadcasted_iota(jnp.int32, (K, K), 1)
    mode = jnp.where(target < K // 2, 2 * target, 2 * target + 1 - K)
    picks = jnp.where(source == mode, 1.0, 0.0).astype(BF16)
    wp_ref[...] = exact_dot(jnp.broadcast_to(w_ref[...], (8, K)), picks)
    copy.wait()

    def body(a, carry):
        f = table[0:B, :] * table[pl.ds(2 * B + a, 1), :] - table[B : 2 * B, :] * table[pl.ds(2 * B + A + a, 1), :]
        hi, lo = split(f)
        rows = pl.ds(pl.multiple_of(a * B, B), B)
        hi_ref[rows, :] = hi
        lo_ref[rows, :] = lo
        return carry

    lax.fori_loop(0, A, body, 0)


def collide_kernel(g_ref, e_ref, rate_in, wp_ref, hi_ref, lo_ref, out_ref, a_ref, b_ref, r_ref, l_ref, c_ref, m_ref, s_ref):
    blocks, rows, _ = g_ref.shape
    wide = rows // 2
    own = wide - 4
    pad = 48
    half = K // 2
    chunks = H // 128
    lane = lax.broadcasted_iota(jnp.int32, (1, 128), 1)
    spot = place(blocks)
    r_ref[...] = rate_in[...]

    def given(n):
        return g_ref[n // 2, (n % 2) * wide : (n % 2 + 1) * wide, :]

    for n in range(2 * chunks):
        b_ref[n, 0:wide, :] = given(n)

    def outer(first):
        for n in range(2 * chunks):
            mine = b_ref[n, 0:4, :] if first else b_ref[n, own:wide, :]
            other = e_ref[4 * n : 4 * n + 4, :]
            s_ref[n, 0:4, :] = other if first else mine
            s_ref[n, 4:8, :] = mine if first else other
            speed = jnp.abs(courant_row(lane + n * 128))
            new = advect(lambda k: s_ref[n, 2 + k : 6 + k, :], speed, n >= chunks)
            if first:
                b_ref[n, 0:4, :] = new
            else:
                b_ref[n, own:wide, :] = new
        if first:
            r_ref[0:2, :] = e_ref[8 * blocks + 2 : 8 * blocks + 4, :]
        else:
            r_ref[own + 2 : wide, :] = e_ref[8 * blocks : 8 * blocks + 2, :]

    @pl.when(spot == 0)
    def _():
        outer(True)

    @pl.when(spot == blocks - 1)
    def _():
        outer(False)

    def fold(c, up, down, at):
        count = up.shape[0]
        for part, first in ((up + down, c * 128), (up - down, H + c * 128)):
            hi, lo = split(part)
            l_ref[0:count, first : first + 128] = hi
            l_ref[at : at + count, first : first + 128] = lo

    def correction(count, at):
        for s in range(2):
            modes = slice(s * half, (s + 1) * half)
            left = l_ref[: 2 * at, s * H : (s + 1) * H]
            both = dot(left, hi_ref[:, modes])
            coef = both[:count] + both[at : at + count] + dot(left[:at], lo_ref[:, modes])[:count]
            hi, lo = split(coef * wp_ref[0:1, modes])
            m_ref[0:count, modes] = hi
            m_ref[at : at + count, modes] = lo
            right = m_ref[: 2 * at, modes]
            back = dot_t(right, hi_ref[:, modes])
            c_ref[:count, s * H : (s + 1) * H] = (
                back[:count] + back[at : at + count] + dot_t(right[:at], lo_ref[:, modes])[:count]
            )

    def corrections(count, c):
        even = c_ref[:count, c * 128 : (c + 1) * 128]
        odd = c_ref[:count, H + c * 128 : H + (c + 1) * 128]
        return even + odd, even - odd

    for c in range(chunks):
        down = mirrored(b_ref[2 * chunks - 1 - c, 0:wide, :])
        a_ref[chunks + c, 0:wide, :] = down
        fold(c, b_ref[c, 0:wide, :], down, pad)
    correction(wide, pad)
    rate = r_ref[...]
    for c in range(chunks):
        plus, minus = corrections(wide, c)
        a_ref[c, 0:wide, :] = b_ref[c, 0:wide, :] - rate * plus
        a_ref[chunks + c, 0:wide, :] = a_ref[chunks + c, 0:wide, :] - rate * minus
        speed = jnp.abs(courant_row(lane + c * 128))
        up = advect(lambda k: a_ref[c, 2 + k : 2 + k + own, :], speed, False)
        down = advect(lambda k: a_ref[chunks + c, 2 + k : 2 + k + own, :], speed, True)
        b_ref[c, 0:own, :] = up
        b_ref[chunks + c, 0:own, :] = down
        fold(c, up, down, own)
    correction(own, own)
    rate = r_ref[2 : own + 2, :]
    for c in range(chunks):
        plus, minus = corrections(own, c)
        n = 2 * chunks - 1 - c
        out_ref[c // 2, :, (c % 2) * 128 : (c % 2 + 1) * 128] = b_ref[c, 0:own, :] - rate * plus
        out_ref[n // 2, :, (n % 2) * 128 : (n % 2 + 1) * 128] = mirrored(
            b_ref[chunks + c, 0:own, :] - rate * minus
        )


def unflip_kernel(t_ref, out_ref):
    blocks, own, _ = t_ref.shape
    odd = lax.rem(lax.axis_index("space"), 2)
    order = [odd] + [p + 1 for p in range(1, blocks - 1)] + [1 - odd]
    per = 128 // own
    for p in range(blocks // per):
        rows = jnp.concatenate([t_ref[r] for r in order[p * per : (p + 1) * per]], axis=0)
        out_ref[:, p * 128 : (p + 1) * 128] = rows.T


def params(mib):
    return pltpu.CompilerParams(vmem_limit_bytes=mib * 1024 * 1024)


VMEM = pl.BlockSpec(memory_space=pltpu.VMEM)
SMEM = pl.BlockSpec(memory_space=pltpu.SMEM)
ANY = pl.BlockSpec(memory_space=pl.ANY)


def shards(distribution, cell_kind, type_rates, mode_weights):
    nv, nx = distribution.shape
    blocks = lax.axis_size("vel")
    slabs = lax.axis_size("space")
    own = nx // blocks
    wide = own + 4
    sent = pl.pallas_call(
        functools.partial(flip_kernel, blocks),
        out_shape=jax.ShapeDtypeStruct((blocks, nv // 128 * wide, 128), F32),
        in_specs=[ANY],
        out_specs=VMEM,
        scratch_shapes=[
            pltpu.VMEM((nv, nx), F32),
            pltpu.VMEM((nv // 128, nx + 16, 128), F32),
            pltpu.SemaphoreType.DMA((nx // 128,)),
        ],
        compiler_params=params(8),
        name="flip",
    )(distribution)
    got = lax.all_to_all(sent, "vel", 0, 0, tiled=True)
    rate, rate_edge = pl.pallas_call(
        functools.partial(rate_kernel, blocks),
        out_shape=(
            jax.ShapeDtypeStruct((wide, 128), F32),
            jax.ShapeDtypeStruct((8, 128), F32),
        ),
        in_specs=[SMEM, VMEM],
        out_specs=(VMEM, VMEM),
        scratch_shapes=[pltpu.VMEM((nx + 16, 128), F32)],
        compiler_params=params(8),
        name="rates",
    )(type_rates[None, :], cell_kind[None, :])
    edge = pl.pallas_call(
        edge_kernel,
        out_shape=jax.ShapeDtypeStruct((8 * blocks + 8, 128), F32),
        in_specs=[VMEM, VMEM],
        out_specs=VMEM,
        compiler_params=params(8),
        name="edges",
    )(got, rate_edge)
    pairs = []
    for s in range(slabs):
        after = (s + 1) % slabs
        rank = 1 - s % 2
        pairs += [(rank * slabs + s, rank * slabs + after), (rank * slabs + after, rank * slabs + s)]
    edge_in = lax.ppermute(edge, ("vel", "space"), pairs)
    hi, lo, weights = pl.pallas_call(
        factor_kernel,
        out_shape=(
            jax.ShapeDtypeStruct((H, K), BF16),
            jax.ShapeDtypeStruct((H, K), BF16),
            jax.ShapeDtypeStruct((8, K), F32),
        ),
        in_specs=[ANY, VMEM, ANY],
        out_specs=(VMEM, VMEM, VMEM),
        scratch_shapes=[pltpu.VMEM((2 * (A + B), K), F32), pltpu.SemaphoreType.DMA],
        compiler_params=params(12),
        name="factors",
    )(jnp.asarray(tables()), mode_weights[None, :], edge)
    back = pl.pallas_call(
        collide_kernel,
        out_shape=jax.ShapeDtypeStruct((blocks, own, nv), F32),
        in_specs=[VMEM] * 6,
        out_specs=VMEM,
        scratch_shapes=[
            pltpu.VMEM((V // 128, wide + 4, 128), F32),
            pltpu.VMEM((V // 128, wide + 4, 128), F32),
            pltpu.VMEM((wide, 128), F32),
            pltpu.VMEM((96, V), BF16),
            pltpu.VMEM((wide + 4, V), F32),
            pltpu.VMEM((96, K), BF16),
            pltpu.VMEM((V // 128, 8, 128), F32),
        ],
        compiler_params=params(24),
        name="collide",
    )(got, edge_in, rate, weights, hi, lo)
    result = lax.all_to_all(back, "vel", 0, 0, tiled=True)
    return pl.pallas_call(
        unflip_kernel,
        out_shape=jax.ShapeDtypeStruct((nv, nx), F32),
        in_specs=[VMEM],
        out_specs=VMEM,
        compiler_params=params(8),
        name="unflip",
    )(result)


def solution(mesh):
    return jax.shard_map(
        shards,
        mesh=mesh,
        in_specs=(P("vel", "space"), P("space"), P(), P()),
        out_specs=P("vel", "space"),
        check_vma=False,
    )
```

time: 76 us -> 70.8 us (0.932)
  waiting for transfers between devices: 17.3 us -> 12.3 us
  blocking collectives: 26.7 us -> 28.5 us
  local copies, waits for them, and re-layouts: 2.41 us -> 1.06 us
    ppermute x1, waiting for transfers between devices: 4.14 us -> 0.01 us  [shards(): edge_in = lax.ppermute(edge, ('vel', 'space'), pairs)]
    all_to_all x1, blocking collectives: 26.7 us -> 28.5 us  [shards(): result = lax.all_to_all(back, 'vel', 0, 0, tiled=True)]
    unnamed x10, local copies, waits for them, and re-layouts: 2.4 us -> 1.06 us
    pallas_call x1, Pallas kernels: 6.2 us -> 5.17 us  [shards(): pl.pallas_call(collide_kernel, out_shape=jax.ShapeDtypeStruct((blocks, ow...]
    all_to_all x1, waiting for transfers between devices: 13.1 us -> 12.3 us  [shards(): got = lax.all_to_all(sent, 'vel', 0, 0, tiled=True)]
    pallas_call x1 -> x3, Pallas kernels: 2.05 us -> 2.42 us  [the longest x1 1.72 us: shards(): pl.pallas_call(functools.partial(flip_kernel, blocks), out_shape=jax.Shap...]
  transfers between devices with their start and end apart: 2 -> 2, of which waited for: 2 -> 1; matrix products, arithmetic and copies ran while one was open for 0% -> 0% of each run, Pallas kernels for 2% -> 3%
where the time goes in v3:
time: 70.8 us; the launch traced here: 70.5 us
  blocking collectives  28.5 us (40%)
  starting transfers between devices  18.4 us (26%)
  waiting for transfers between devices  12.3 us (17%)
  Pallas kernels  10.2 us (14%)
  local copies, waits for them, and re-layouts  1.06 us (1%)
    all_to_all x1, blocking collectives, shards(): result = lax.all_to_all(back, 'vel', 0, 0, tiled=True)  28.5 us
    all_to_all x1, starting transfers between devices, shards(): got = lax.all_to_all(sent, 'vel', 0, 0, tiled=True)  16.5 us
    all_to_all x1, waiting for transfers between devices, shards(): got = lax.all_to_all(sent, 'vel', 0, 0, tiled=True)  12.3 us
    pallas_call x1, Pallas kernels, shards(): pl.pallas_call(collide_kernel, out_shape=jax.ShapeDtypeStruct((blocks, ow...  5.17 us
    ppermute x1, starting transfers between devices, shards(): edge_in = lax.ppermute(edge, ('vel', 'space'), pairs)  1.92 us
    pallas_call x1, Pallas kernels, shards(): pl.pallas_call(functools.partial(flip_kernel, blocks), out_shape=jax.Shap...  1.72 us
    pallas_call x1, Pallas kernels, shards(): pl.pallas_call(factor_kernel, out_shape=(jax.ShapeDtypeStruct((H, K), BF1...  1.6 us
  transfers between devices with their start and end apart: 2, of which 1 were waited for; matrix products, arithmetic and copies ran while one was open for 0% of the time, Pallas kernels for 3%

profile of v3, /device:TPU:8, one launch (start us, length us, event | category | flops | bytes accessed | tf_op | source)
XLA Modules:
  0.0 70.5 jit_solution(10427535948111136211)
XLA Ops:
  0.0 0.0 copy-start
  0.0 1.0 %copy-done = f32[256,512]{1,0:T(8,128)S(1)} copy-done((f32[256,512]{1,0:T(8,128)S(1)}, f32[256,512]{1,0:T(8,128)}, u32[]{:S(2)}) %copy-start) | copy-done | bytes 524312
  1.0 0.0 copy-start.3
  1.0 0.0 copy-start.4
  1.0 0.0 copy-start.1
  1.0 0.0 copy-start.2
  1.1 1.7 %flip.1 = f32[16,72,128]{2,1,0:T(8,128)} custom-call(f32[256,512]{1,0:T(8,128)S(1)} %copy-done), custom_call_target="tpu_custom_call" | custom-call | tf_op jit(solution)/shard_map/flip/pallas_call | solution.py:307
  2.8 16.5 %all-to-all-start = ((f32[16,72,128]{2,1,0:T(8,128)}), f32[16,72,128]{2,1,0:T(8,128)S(1)}, u32[]{:S(2)}, u32[]{:S(2)}) async-start(f32[16,72,128]{2,1,0:T(8,128)} %flip.1), calls=%async_computation | async-start | bytes 1179648 | tf_op jit(solution)/shard_map/all_to_all | solution.py:320
  19.2 0.0 copy-done.3
  19.2 0.0 copy-done.4
  19.2 0.7 rates.1
  19.9 12.3 %all-to-all-done.g_ref = f32[16,72,128]{2,1,0:T(8,128)S(1)} async-done(((f32[16,72,128]{2,1,0:T(8,128)}), f32[16,72,128]{2,1,0:T(8,128)S(1)}, u32[]{:S(2)}, u32[]{:S(2)}) %all-to-all-start) | async-done | bytes 589856 | tf_op jit(solution)/shard_map/all_to_all | solution.py:320
  32.3 1.9 %collective-permute-start = (f32[136,128]{1,0:T(8,128)S(1)}, f32[136,128]{1,0:T(8,128)S(1)}, u32[]{:S(2)}, u32[]{:S(2)}) collective-permute-start(f32[136,128]{1,0:T(8,128)S(1)} %edges.1.edge_hbm), channel_id=1, source_target_pairs={{64,65},{65,64},{1,2},{2,1},{66,67},{67,66},{3,4},{4,3},{68,69},{6... | collective-permute-start | bytes 208904 | tf_op jit(solution)/shard_map/ppermute | solution.py:346
  34.2 0.0 copy-done.1
  34.2 0.0 copy-done.2
  34.2 1.6 %factors.1 = (bf16[2048,512]{1,0:T(8,128)(2,1)S(1)}, bf16[2048,512]{1,0:T(8,128)(2,1)S(1)}, f32[8,512]{1,0:T(8,128)S(1)}) custom-call(f32[192,512]{1,0:T(8,128)S(1)} %copy-done.1, f32[1,512]{1,0:T(1,128)S(1)} %bitcast.3, f32[136,128]{1,0:T(8,128)S(1)} %edges.1.edge_hbm), custom_call_target="tpu_custom_call" | custom-call | tf_op jit(solution)/shard_map/factors/pallas_call | solution.py:347
  35.9 0.0 collective-permute-done.e_ref
  35.9 5.2 %collide.1 = f32[16,32,256]{2,1,0:T(8,128)S(1)} custom-call(f32[16,72,128]{2,1,0:T(8,128)S(1)} %all-to-all-done.g_ref, f32[136,128]{1,0:T(8,128)S(1)} %collective-permute-done.e_ref, f32[36,128]{1,0:T(8,128)S(1)} %get-tuple-element.11.rate_in, f32[8,512]{1,0:T(8,128)S(1)} %get-tuple-element.12.wp_ref, bf16[2048,512]{1,0:T(8,128)(2,1)S(1)} %get-tuple-element.13.hi_ref, ...), custom_call_target="tpu_custom_call" | custom-call | tf_op jit(solution)/shard_map/collide/pallas_call | solution.py:360
  41.0 28.5 %all_to_all.10.t_ref = f32[16,32,256]{2,1,0:T(8,128)S(1)} all-to-all(f32[16,32,256]{2,1,0:T(8,128)S(1)} %collide.1), channel_id=1, replica_groups=mesh['vel'=16,'space'=64] {'vel'}, dimensions={0} | all-to-all | bytes 1048576 | tf_op jit(solution)/shard_map/all_to_all | solution.py:377
  69.5 1.0 %unflip.1 = f32[256,512]{1,0:T(8,128)} custom-call(f32[16,32,256]{2,1,0:T(8,128)S(1)} %all_to_all.10.t_ref), custom_call_target="tpu_custom_call" | custom-call | tf_op jit(solution)/shard_map/unflip/pallas_call | solution.py:378
  (1 shorter events, 0.0 us)
Async XLA Ops:
  0.0 1.0 %copy-start = (f32[256,512]{1,0:T(8,128)S(1)}, f32[256,512]{1,0:T(8,128)}, u32[]{:S(2)}) copy-start(f32[256,512]{1,0:T(8,128)} %f_hbm.1) | copy-start | bytes 1572868
  1.0 18.2 %copy-start.3 = (s32[512]{0:T(512)S(1)}, s32[512]{0:T(512)}, u32[]{:S(2)}) copy-start(s32[512]{0:T(512)} %param.6) | copy-start | bytes 6148
  1.0 18.2 %copy-start.4 = (f32[4]{0:T(128)S(1)}, f32[4]{0:T(128)}, u32[]{:S(2)}) copy-start(f32[4]{0:T(128)} %param.7) | copy-start | bytes 52
  1.0 33.2 %copy-start.1 = (f32[192,512]{1,0:T(8,128)S(1)}, f32[192,512]{1,0:T(8,128)}, u32[]{:S(2)}) copy-start(f32[192,512]{1,0:T(8,128)} %constant.2.clone.table_hbm) | copy-start | bytes 1179652
  1.0 33.2 %copy-start.2 = (f32[512]{0:T(512)S(1)}, f32[512]{0:T(512)}, u32[]{:S(2)}) copy-start(f32[512]{0:T(512)} %param.8) | copy-start | bytes 6148
  2.8 29.5 %all-to-all-start = ((f32[16,72,128]{2,1,0:T(8,128)}), f32[16,72,128]{2,1,0:T(8,128)S(1)}, u32[]{:S(2)}, u32[]{:S(2)}) async-start(f32[16,72,128]{2,1,0:T(8,128)} %flip.1), calls=%async_computation | async-start | bytes 1179648 | tf_op jit(solution)/shard_map/all_to_all | solution.py:320
  32.3 3.6 %collective-permute-start = (f32[136,128]{1,0:T(8,128)S(1)}, f32[136,128]{1,0:T(8,128)S(1)}, u32[]{:S(2)}, u32[]{:S(2)}) collective-permute-start(f32[136,128]{1,0:T(8,128)S(1)} %edges.1.edge_hbm), channel_id=1, source_target_pairs={{64,65},{65,64},{1,2},{2,1},{66,67},{67,66},{3,4},{4,3},{68,69},{6... | collective-permute-start | bytes 208904 | tf_op jit(solution)/shard_map/ppermute | solution.py:346

commit v4 on v3

--- a/solution.py
+++ b/solution.py
@@ -50,10 +50,7 @@
 
 
 def minmod(a, b):
-    zero = jnp.zeros_like(a)
-    return jnp.minimum(jnp.maximum(a, zero), jnp.maximum(b, zero)) + jnp.maximum(
-        jnp.minimum(a, zero), jnp.minimum(b, zero)
-    )
+    return jnp.maximum(jnp.minimum(a, b), jnp.minimum(jnp.maximum(a, b), 0.0))
 
 
 def upwind(far, near, here, other, speed):
@@ -84,7 +81,7 @@
     return jnp.where(me > 1, me - 1, jnp.where(me == odd, 0, blocks - 1))
 
 
-def flip_kernel(blocks, f_hbm, out_ref, f_ref, ext, sems):
+def flip_kernel(blocks, f_hbm, out_hbm, f_ref, ext, out_ref, sems, out_sems):
     me = lax.axis_index("vel")
     odd = lax.rem(lax.axis_index("space"), 2)
     nv, nx = f_ref.shape
@@ -103,22 +100,24 @@
     ahead = me >= blocks // 2
     speeds = [jnp.abs(courant_row(me * nv + h * 128 + lane)) for h in range(nv // 128)]
 
-    def make(p, r):
+    def rank_of(p):
+        return odd if p == 0 else 1 - odd if p == blocks - 1 else p + 1
+
+    def make(p, positive):
+        r = rank_of(p)
         for h in range(nv // 128):
             base = 8 + p * own - 2
-
-            def at(k, base=base, h=h):
-                return ext[h, base + k : base + k + wide, :]
-
-            below, above = at(-1), at(1)
-            near = jnp.where(ahead, below, above)
-            other = jnp.where(ahead, above, below)
-            far = jnp.where(ahead, at(-2), at(2))
-            out_ref[r, h * wide : (h + 1) * wide, :] = upwind(far, near, at(0), other, speeds[h])
+            out_ref[r, h * wide : (h + 1) * wide, :] = advect(
+                lambda k: ext[h, base + k : base + k + wide, :], speeds[h], positive
+            )
             if p == 0:
                 out_ref[r, h * wide : h * wide + 4, :] = ext[h, 8:12, :]
             if p == blocks - 1:
                 out_ref[r, h * wide + own : (h + 1) * wide, :] = ext[h, nx + 4 : nx + 8, :]
+
+    def send(p):
+        r = rank_of(p)
+        return pltpu.make_async_copy(out_ref.at[r], out_hbm.at[r], out_sems.at[p])
 
     done = 0
     for p in range(parts):
@@ -127,9 +126,19 @@
             ext[h, 8 + p * 128 : 8 + (p + 1) * 128, :] = f_ref[
                 h * 128 : (h + 1) * 128, p * 128 : (p + 1) * 128
             ].T
-        while done < blocks and (done == 0 or (done + 1) * own + 4 <= (p + 1) * 128 or p == parts - 1):
-            make(done, odd if done == 0 else 1 - odd if done == blocks - 1 else done + 1)
-            done += 1
+        ready = blocks if p == parts - 1 else ((p + 1) * 128 - 4) // own
+        for positive in (False, True):
+
+            @pl.when(ahead == positive)
+            def _(begin=done, positive=positive, ready=ready):
+                for window in range(begin, ready):
+                    make(window, positive)
+
+        for window in range(done, ready):
+            send(window).start()
+        done = ready
+    for window in range(blocks):
+        send(window).wait()
 
 
 def rate_kernel(blocks, rates_ref, kind_ref, rate_ref, edge_ref, ext):
@@ -279,14 +288,20 @@
         )
 
 
-def unflip_kernel(t_ref, out_ref):
+def unflip_kernel(t_ref, out_hbm, out_ref, sems):
     blocks, own, _ = t_ref.shape
     odd = lax.rem(lax.axis_index("space"), 2)
     order = [odd] + [p + 1 for p in range(1, blocks - 1)] + [1 - odd]
     per = 128 // own
+    copies = []
     for p in range(blocks // per):
+        columns = slice(p * 128, (p + 1) * 128)
         rows = jnp.concatenate([t_ref[r] for r in order[p * per : (p + 1) * per]], axis=0)
-        out_ref[:, p * 128 : (p + 1) * 128] = rows.T
+        out_ref[:, columns] = rows.T
+        copies.append(pltpu.make_async_copy(out_ref.at[:, columns], out_hbm.at[:, columns], sems.at[p]))
+        copies[-1].start()
+    for copy in copies:
+        copy.wait()
 
 
 def params(mib):
@@ -308,15 +323,17 @@
         functools.partial(flip_kernel, blocks),
         out_shape=jax.ShapeDtypeStruct((blocks, nv // 128 * wide, 128), F32),
         in_specs=[ANY],
-        out_specs=VMEM,
+        out_specs=ANY,
         scratch_shapes=[
             pltpu.VMEM((nv, nx), F32),
             pltpu.VMEM((nv // 128, nx + 16, 128), F32),
+            pltpu.VMEM((blocks, nv // 128 * wide, 128), F32),
             pltpu.SemaphoreType.DMA((nx // 128,)),
+            pltpu.SemaphoreType.DMA((blocks,)),
         ],
         compiler_params=params(8),
         name="flip",
-    )(distribution)
+    )(pltpu.with_memory_space_constraint(distribution, pltpu.MemorySpace.HBM))
     got = lax.all_to_all(sent, "vel", 0, 0, tiled=True)
     rate, rate_edge = pl.pallas_call(
         functools.partial(rate_kernel, blocks),
@@ -379,7 +396,8 @@
         unflip_kernel,
         out_shape=jax.ShapeDtypeStruct((nv, nx), F32),
         in_specs=[VMEM],
-        out_specs=VMEM,
+        out_specs=ANY,
+        scratch_shapes=[pltpu.VMEM((nv, nx), F32), pltpu.SemaphoreType.DMA((nx // 128,))],
         compiler_params=params(8),
         name="unflip",
     )(result)

time: 70.8 us -> 70.5 us (level)
  local copies, waits for them, and re-layouts: 1.06 us -> 0.02 us
    unnamed x10 -> x8, local copies, waits for them, and re-layouts: 1.06 us -> 0.02 us
    pallas_call x1, Pallas kernels: 1.72 us -> 2.56 us  [shards(): pl.pallas_call(functools.partial(flip_kernel, blocks), out_shape=jax.Shap...]
where the time goes in v4:
time: 70.5 us; the launch traced here: 70.3 us
  blocking collectives  28.5 us (40%)
  starting transfers between devices  18.4 us (26%)
  waiting for transfers between devices  12.3 us (17%)
  Pallas kernels  10.9 us (15%)
    all_to_all x1, blocking collectives, shards(): result = lax.all_to_all(back, 'vel', 0, 0, tiled=True)  28.5 us
    all_to_all x1, starting transfers between devices, shards(): got = lax.all_to_all(sent, 'vel', 0, 0, tiled=True)  16.4 us
    all_to_all x1, waiting for transfers between devices, shards(): got = lax.all_to_all(sent, 'vel', 0, 0, tiled=True)  12.3 us
    pallas_call x1, Pallas kernels, shards(): pl.pallas_call(collide_kernel, out_shape=jax.ShapeDtypeStruct((blocks, ow...  5.15 us
    pallas_call x1, Pallas kernels, shards(): pl.pallas_call(functools.partial(flip_kernel, blocks), out_shape=jax.Shap...  2.56 us
    ppermute x1, starting transfers between devices, shards(): edge_in = lax.ppermute(edge, ('vel', 'space'), pairs)  1.92 us
    pallas_call x1, Pallas kernels, shards(): pl.pallas_call(factor_kernel, out_shape=(jax.ShapeDtypeStruct((H, K), BF1...  1.6 us
  transfers between devices with their start and end apart: 2, of which 1 were waited for; matrix products, arithmetic and copies ran while one was open for 0% of the time, Pallas kernels for 3%

profile of v4, /device:TPU:8, one launch (start us, length us, event | category | flops | bytes accessed | tf_op | source)
XLA Modules:
  0.0 70.3 jit_solution(11157033441257741135)
XLA Ops:
  0.0 0.0 copy-start
  0.0 0.0 copy-start.3
  0.0 0.0 copy-start.2
  0.0 0.0 copy-start.1
  0.0 2.6 %flip.1 = f32[16,72,128]{2,1,0:T(8,128)} custom-call(f32[256,512]{1,0:T(8,128)} %f_hbm.1), custom_call_target="tpu_custom_call" | custom-call | tf_op jit(solution)/shard_map/flip/pallas_call | solution.py:322
  2.6 16.4 %all-to-all-start = ((f32[16,72,128]{2,1,0:T(8,128)}), f32[16,72,128]{2,1,0:T(8,128)S(1)}, u32[]{:S(2)}, u32[]{:S(2)}) async-start(f32[16,72,128]{2,1,0:T(8,128)} %flip.1), calls=%async_computation | async-start | bytes 1179648 | tf_op jit(solution)/shard_map/all_to_all | solution.py:337
  19.0 0.0 copy-done.3
  19.0 0.0 copy-done.2
  19.0 0.7 rates.1
  19.7 12.3 %all-to-all-done.g_ref = f32[16,72,128]{2,1,0:T(8,128)S(1)} async-done(((f32[16,72,128]{2,1,0:T(8,128)}), f32[16,72,128]{2,1,0:T(8,128)S(1)}, u32[]{:S(2)}, u32[]{:S(2)}) %all-to-all-start) | async-done | bytes 589856 | tf_op jit(solution)/shard_map/all_to_all | solution.py:337
  32.1 1.9 %collective-permute-start = (f32[136,128]{1,0:T(8,128)S(1)}, f32[136,128]{1,0:T(8,128)S(1)}, u32[]{:S(2)}, u32[]{:S(2)}) collective-permute-start(f32[136,128]{1,0:T(8,128)S(1)} %edges.1.edge_hbm), channel_id=1, source_target_pairs={{64,65},{65,64},{1,2},{2,1},{66,67},{67,66},{3,4},{4,3},{68,69},{6... | collective-permute-start | bytes 208904 | tf_op jit(solution)/shard_map/ppermute | solution.py:363
  34.0 0.0 copy-done
  34.0 0.0 copy-done.1
  34.0 1.6 %factors.1 = (bf16[2048,512]{1,0:T(8,128)(2,1)S(1)}, bf16[2048,512]{1,0:T(8,128)(2,1)S(1)}, f32[8,512]{1,0:T(8,128)S(1)}) custom-call(f32[192,512]{1,0:T(8,128)S(1)} %copy-done, f32[1,512]{1,0:T(1,128)S(1)} %bitcast.3, f32[136,128]{1,0:T(8,128)S(1)} %edges.1.edge_hbm), custom_call_target="tpu_custom_call" | custom-call | tf_op jit(solution)/shard_map/factors/pallas_call | solution.py:364
  35.7 0.0 collective-permute-done.e_ref
  35.7 5.2 %collide.1 = f32[16,32,256]{2,1,0:T(8,128)S(1)} custom-call(f32[16,72,128]{2,1,0:T(8,128)S(1)} %all-to-all-done.g_ref, f32[136,128]{1,0:T(8,128)S(1)} %collective-permute-done.e_ref, f32[36,128]{1,0:T(8,128)S(1)} %get-tuple-element.11.rate_in, f32[8,512]{1,0:T(8,128)S(1)} %get-tuple-element.12.wp_ref, bf16[2048,512]{1,0:T(8,128)(2,1)S(1)} %get-tuple-element.13.hi_ref, ...), custom_call_target="tpu_custom_call" | custom-call | tf_op jit(solution)/shard_map/collide/pallas_call | solution.py:377
  40.8 28.5 %all_to_all.10.t_ref = f32[16,32,256]{2,1,0:T(8,128)S(1)} all-to-all(f32[16,32,256]{2,1,0:T(8,128)S(1)} %collide.1), channel_id=1, replica_groups=mesh['vel'=16,'space'=64] {'vel'}, dimensions={0} | all-to-all | bytes 1048576 | tf_op jit(solution)/shard_map/all_to_all | solution.py:394
  69.3 0.9 %unflip.1 = f32[256,512]{1,0:T(8,128)} custom-call(f32[16,32,256]{2,1,0:T(8,128)S(1)} %all_to_all.10.t_ref), custom_call_target="tpu_custom_call" | custom-call | tf_op jit(solution)/shard_map/unflip/pallas_call | solution.py:395
  (1 shorter events, 0.0 us)
Async XLA Ops:
  0.0 34.0 %copy-start = (f32[192,512]{1,0:T(8,128)S(1)}, f32[192,512]{1,0:T(8,128)}, u32[]{:S(2)}) copy-start(f32[192,512]{1,0:T(8,128)} %constant.2.clone.table_hbm) | copy-start | bytes 1179652
  0.0 19.0 %copy-start.3 = (f32[4]{0:T(128)S(1)}, f32[4]{0:T(128)}, u32[]{:S(2)}) copy-start(f32[4]{0:T(128)} %param.7) | copy-start | bytes 52
  0.0 19.0 %copy-start.2 = (s32[512]{0:T(512)S(1)}, s32[512]{0:T(512)}, u32[]{:S(2)}) copy-start(s32[512]{0:T(512)} %param.6) | copy-start | bytes 6148
  0.0 34.0 %copy-start.1 = (f32[512]{0:T(512)S(1)}, f32[512]{0:T(512)}, u32[]{:S(2)}) copy-start(f32[512]{0:T(512)} %param.8) | copy-start | bytes 6148
  2.6 29.5 %all-to-all-start = ((f32[16,72,128]{2,1,0:T(8,128)}), f32[16,72,128]{2,1,0:T(8,128)S(1)}, u32[]{:S(2)}, u32[]{:S(2)}) async-start(f32[16,72,128]{2,1,0:T(8,128)} %flip.1), calls=%async_computation | async-start | bytes 1179648 | tf_op jit(solution)/shard_map/all_to_all | solution.py:337
  32.1 3.6 %collective-permute-start = (f32[136,128]{1,0:T(8,128)S(1)}, f32[136,128]{1,0:T(8,128)S(1)}, u32[]{:S(2)}, u32[]{:S(2)}) collective-permute-start(f32[136,128]{1,0:T(8,128)S(1)} %edges.1.edge_hbm), channel_id=1, source_target_pairs={{64,65},{65,64},{1,2},{2,1},{66,67},{67,66},{3,4},{4,3},{68,69},{6... | collective-permute-start | bytes 208904 | tf_op jit(solution)/shard_map/ppermute | solution.py:363

commit v5 on v4

--- a/solution.py
+++ b/solution.py
@@ -28,6 +28,19 @@
     return np.concatenate(parts).astype(np.float32)
 
 
+D = 16
+
+
+def mode_tables():
+    v = 2 * np.arange(H) + 1
+    rows = []
+    for modes in (2 * np.arange(D), 2 * np.arange(D) + 1, 2 * D * np.arange(K // (2 * D))):
+        angle = modes[:, None] * v[None, :] % (4 * V) * (math.pi / (2 * V))
+        scale = math.sqrt(2.0 / V) if len(rows) < 4 else 1.0
+        rows += [np.cos(angle) * scale, np.sin(angle) * scale]
+    return np.concatenate(rows).astype(np.float32)
+
+
 def split(x):
     hi = x.astype(BF16)
     return hi, (x - hi.astype(F32)).astype(BF16)
@@ -35,10 +48,6 @@
 
 def dot(a, b):
     return lax.dot_general(a, b, (((1,), (0,)), ((), ())), preferred_element_type=F32)
-
-
-def dot_t(a, b):
-    return lax.dot_general(a, b, (((1,), (1,)), ((), ())), preferred_element_type=F32)
 
 
 def exact_dot(x, picks):
@@ -156,7 +165,7 @@
     edge_ref[...] = jnp.where(spot == 0, ext[8:16, :], ext[nx + 4 : nx + 12, :])
 
 
-def edge_kernel(g_ref, rate_ref, out_ref):
+def edge_kernel(g_ref, rate_ref, token_ref, out_ref):
     blocks, rows, _ = g_ref.shape
     wide = rows // 2
     first = place(blocks) == 0
@@ -171,6 +180,42 @@
     out_ref[8 * blocks :, :] = rate_ref[...]
 
 
+def mode_factor_kernel(table_hbm, sent_hbm, hi_hbm, lo_hbm, token_ref, hi_ref, lo_ref, table, sem, sems):
+    token_ref[...] = jnp.zeros_like(token_ref)
+    copy = pltpu.make_async_copy(table_hbm, table, sem)
+    copy.start()
+    copy.wait()
+    row = lax.broadcasted_iota(jnp.int32, (D, 1), 0)
+
+    def block(s, c, weight):
+        near = 2 * D * s
+        f = table[near : near + D, :] * table[pl.ds(4 * D + c, 1), :] - table[
+            near + D : near + 2 * D, :
+        ] * table[pl.ds(4 * D + K // (2 * D) + c, 1), :]
+        if weight is not None:
+            f = f * weight
+        hi, lo = split(f)
+        rows = pl.ds(pl.multiple_of(s * (K // 2) + c * D, D), D)
+        hi_ref[rows, :] = hi
+        lo_ref[rows, :] = lo
+
+    def body(c, carry):
+        block(0, c, None)
+        block(1, c, None)
+        return carry
+
+    lax.fori_loop(0, K // (2 * D), body, 0)
+    block(0, 0, jnp.where(row == 0, math.sqrt(0.5), 1.0))
+    stores = [
+        pltpu.make_async_copy(hi_ref, hi_hbm, sems.at[0]),
+        pltpu.make_async_copy(lo_ref, lo_hbm, sems.at[1]),
+    ]
+    for store in stores:
+        store.start()
+    for store in stores:
+        store.wait()
+
+
 def factor_kernel(table_hbm, w_ref, edge_hbm, hi_ref, lo_ref, wp_ref, table, sem):
     copy = pltpu.make_async_copy(table_hbm, table, sem)
     copy.start()
@@ -192,7 +237,10 @@
     lax.fori_loop(0, A, body, 0)
 
 
-def collide_kernel(g_ref, e_ref, rate_in, wp_ref, hi_ref, lo_ref, out_ref, a_ref, b_ref, r_ref, l_ref, c_ref, m_ref, s_ref):
+def collide_kernel(
+    g_ref, e_ref, rate_in, hi_ref, lo_ref, wp_ref, thi_hbm, tlo_hbm,
+    out_ref, a_ref, b_ref, r_ref, l_ref, c_ref, m_ref, s_ref, thi_ref, tlo_ref, sems,
+):
     blocks, rows, _ = g_ref.shape
     wide = rows // 2
     own = wide - 4
@@ -201,6 +249,12 @@
     chunks = H // 128
     lane = lax.broadcasted_iota(jnp.int32, (1, 128), 1)
     spot = place(blocks)
+    loads = []
+    for n in range(4):
+        rows = slice(n // 2 * half, (n // 2 + 1) * half)
+        source, target = ((thi_hbm, thi_ref), (tlo_hbm, tlo_ref))[n % 2]
+        loads.append(pltpu.make_async_copy(source.at[rows, :], target.at[rows, :], sems.at[n]))
+        loads[n].start()
     r_ref[...] = rate_in[...]
 
     def given(n):
@@ -251,9 +305,12 @@
             m_ref[0:count, modes] = hi
             m_ref[at : at + count, modes] = lo
             right = m_ref[: 2 * at, modes]
-            back = dot_t(right, hi_ref[:, modes])
+            if count == wide:
+                loads[2 * s].wait()
+                loads[2 * s + 1].wait()
+            back = dot(right, thi_ref[modes, :])
             c_ref[:count, s * H : (s + 1) * H] = (
-                back[:count] + back[at : at + count] + dot_t(right[:at], lo_ref[:, modes])[:count]
+                back[:count] + back[at : at + count] + dot(right[:at], tlo_ref[modes, :])[:count]
             )
 
     def corrections(count, c):
@@ -347,21 +404,41 @@
         compiler_params=params(8),
         name="rates",
     )(type_rates[None, :], cell_kind[None, :])
+    *by_modes, token = pl.pallas_call(
+        mode_factor_kernel,
+        out_shape=(
+            pltpu.MemorySpace.HBM((K, H), BF16),
+            pltpu.MemorySpace.HBM((K, H), BF16),
+            jax.ShapeDtypeStruct((8, 128), F32),
+        ),
+        in_specs=[ANY, ANY],
+        out_specs=(ANY, ANY, VMEM),
+        scratch_shapes=[
+            pltpu.VMEM((K, H), BF16),
+            pltpu.VMEM((K, H), BF16),
+            pltpu.VMEM((4 * D + K // D, H), F32),
+            pltpu.SemaphoreType.DMA,
+            pltpu.SemaphoreType.DMA((2,)),
+        ],
+        compiler_params=params(16),
+        name="mode_factors",
+    )(jnp.asarray(mode_tables()), sent)
     edge = pl.pallas_call(
         edge_kernel,
         out_shape=jax.ShapeDtypeStruct((8 * blocks + 8, 128), F32),
-        in_specs=[VMEM, VMEM],
+        in_specs=[VMEM, VMEM, VMEM],
         out_specs=VMEM,
         compiler_params=params(8),
         name="edges",
-    )(got, rate_edge)
+    )(got, rate_edge, token)
     pairs = []
     for s in range(slabs):
         after = (s + 1) % slabs
         rank = 1 - s % 2
         pairs += [(rank * slabs + s, rank * slabs + after), (rank * slabs + after, rank * slabs + s)]
     edge_in = lax.ppermute(edge, ("vel", "space"), pairs)
-    hi, lo, weights = pl.pallas_call(
+    by_modes = [pltpu.with_memory_space_constraint(part, pltpu.MemorySpace.HBM) for part in by_modes]
+    factors = pl.pallas_call(
         factor_kernel,
         out_shape=(
             jax.ShapeDtypeStruct((H, K), BF16),
@@ -369,7 +446,7 @@
             jax.ShapeDtypeStruct((8, K), F32),
         ),
         in_specs=[ANY, VMEM, ANY],
-        out_specs=(VMEM, VMEM, VMEM),
+        out_specs=(VMEM,) * 3,
         scratch_shapes=[pltpu.VMEM((2 * (A + B), K), F32), pltpu.SemaphoreType.DMA],
         compiler_params=params(12),
         name="factors",
@@ -377,7 +454,7 @@
     back = pl.pallas_call(
         collide_kernel,
         out_shape=jax.ShapeDtypeStruct((blocks, own, nv), F32),
-        in_specs=[VMEM] * 6,
+        in_specs=[VMEM] * 6 + [ANY] * 2,
         out_specs=VMEM,
         scratch_shapes=[
             pltpu.VMEM((V // 128, wide + 4, 128), F32),
@@ -387,10 +464,13 @@
             pltpu.VMEM((wide + 4, V), F32),
             pltpu.VMEM((96, K), BF16),
             pltpu.VMEM((V // 128, 8, 128), F32),
+            pltpu.VMEM((K, H), BF16),
+            pltpu.VMEM((K, H), BF16),
+            pltpu.SemaphoreType.DMA((4,)),
         ],
         compiler_params=params(24),
         name="collide",
-    )(got, edge_in, rate, weights, hi, lo)
+    )(got, edge_in, rate, *factors, *by_modes)
     result = lax.all_to_all(back, "vel", 0, 0, tiled=True)
     return pl.pallas_call(
         unflip_kernel,

time: 70.5 us -> 70.6 us (level)
  Pallas kernels: 10.9 us -> 14.3 us
  waiting for transfers between devices: 12.3 us -> 8.99 us
    all_to_all x1, waiting for transfers between devices: 12.3 us -> 8.98 us  [shards(): got = lax.all_to_all(sent, 'vel', 0, 0, tiled=True)]
    pallas_call x0 -> x1, Pallas kernels: none -> 3.34 us  [shards(): pl.pallas_call(mode_factor_kernel, out_shape=(pltpu.MemorySpace.HBM((K, H...]
  transfers between devices with their start and end apart: 2 -> 2, of which waited for: 1 -> 1; matrix products, arithmetic and copies ran while one was open for 0% -> 0% of each run, Pallas kernels for 3% -> 8%
where the time goes in v5:
time: 70.6 us; the launch traced here: 70.3 us
  blocking collectives  28.6 us (41%)
  starting transfers between devices  18.4 us (26%)
  Pallas kernels  14.3 us (20%)
  waiting for transfers between devices  8.99 us (13%)
    all_to_all x1, blocking collectives, shards(): result = lax.all_to_all(back, 'vel', 0, 0, tiled=True)  28.6 us
    all_to_all x1, starting transfers between devices, shards(): got = lax.all_to_all(sent, 'vel', 0, 0, tiled=True)  16.4 us
    all_to_all x1, waiting for transfers between devices, shards(): got = lax.all_to_all(sent, 'vel', 0, 0, tiled=True)  8.98 us
    pallas_call x1, Pallas kernels, shards(): pl.pallas_call(collide_kernel, out_shape=jax.ShapeDtypeStruct((blocks, ow...  5.1 us
    pallas_call x1, Pallas kernels, shards(): pl.pallas_call(mode_factor_kernel, out_shape=(pltpu.MemorySpace.HBM((K, H...  3.34 us
    pallas_call x1, Pallas kernels, shards(): pl.pallas_call(functools.partial(flip_kernel, blocks), out_shape=jax.Shap...  2.61 us
    ppermute x1, starting transfers between devices, shards(): edge_in = lax.ppermute(edge, ('vel', 'space'), pairs)  1.92 us
    pallas_call x1, Pallas kernels, shards(): pl.pallas_call(factor_kernel, out_shape=(jax.ShapeDtypeStruct((H, K), BF1...  1.6 us
  transfers between devices with their start and end apart: 2, of which 1 were waited for; matrix products, arithmetic and copies ran while one was open for 0% of the time, Pallas kernels for 8%

profile of v5, /device:TPU:8, one launch (start us, length us, event | category | flops | bytes accessed | tf_op | source)
XLA Modules:
  0.0 70.3 jit_solution(17617973395713120292)
XLA Ops:
  0.0 0.0 copy-start
  0.0 0.0 copy-start.1
  0.0 0.0 copy-start.4
  0.0 0.0 copy-start.3
  0.0 0.0 copy-start.2
  0.0 2.6 %flip.1.sent_hbm = f32[16,72,128]{2,1,0:T(8,128)} custom-call(f32[256,512]{1,0:T(8,128)} %f_hbm.1), custom_call_target="tpu_custom_call" | custom-call | tf_op jit(solution)/shard_map/flip/pallas_call | solution.py:379
  2.6 16.4 %all-to-all-start = ((f32[16,72,128]{2,1,0:T(8,128)}), f32[16,72,128]{2,1,0:T(8,128)S(1)}, u32[]{:S(2)}, u32[]{:S(2)}) async-start(f32[16,72,128]{2,1,0:T(8,128)} %flip.1.sent_hbm), calls=%async_computation | async-start | bytes 1179648 | tf_op jit(solution)/shard_map/all_to_all | solution.py:394
  19.1 0.0 copy-done
  19.1 3.3 %mode_factors.1 = (bf16[512,2048]{1,0:T(8,128)(2,1)}, bf16[512,2048]{1,0:T(8,128)(2,1)}, f32[8,128]{1,0:T(8,128)S(1)}) custom-call(f32[96,2048]{1,0:T(8,128)S(1)} %copy-done, f32[16,72,128]{2,1,0:T(8,128)} %flip.1.sent_hbm), custom_call_target="tpu_custom_call" | custom-call | tf_op jit(solution)/shard_map/mode_factors/pallas_call | solution.py:407
  22.4 0.0 copy-done.4
  22.4 0.0 copy-done.3
  22.5 0.7 rates.1
  23.1 9.0 %all-to-all-done.g_ref = f32[16,72,128]{2,1,0:T(8,128)S(1)} async-done(((f32[16,72,128]{2,1,0:T(8,128)}), f32[16,72,128]{2,1,0:T(8,128)S(1)}, u32[]{:S(2)}, u32[]{:S(2)}) %all-to-all-start) | async-done | bytes 589856 | tf_op jit(solution)/shard_map/all_to_all | solution.py:394
  32.2 1.9 %collective-permute-start = (f32[136,128]{1,0:T(8,128)S(1)}, f32[136,128]{1,0:T(8,128)S(1)}, u32[]{:S(2)}, u32[]{:S(2)}) collective-permute-start(f32[136,128]{1,0:T(8,128)S(1)} %edges.1.edge_hbm), channel_id=1, source_target_pairs={{64,65},{65,64},{1,2},{2,1},{66,67},{67,66},{3,4},{4,3},{68,69},{6... | collective-permute-start | bytes 208904 | tf_op jit(solution)/shard_map/ppermute | solution.py:439
  34.1 0.0 copy-done.1
  34.1 0.0 copy-done.2
  34.1 1.6 %factors.1 = (bf16[2048,512]{1,0:T(8,128)(2,1)S(1)}, bf16[2048,512]{1,0:T(8,128)(2,1)S(1)}, f32[8,512]{1,0:T(8,128)S(1)}) custom-call(f32[192,512]{1,0:T(8,128)S(1)} %copy-done.1, f32[1,512]{1,0:T(1,128)S(1)} %bitcast.3, f32[136,128]{1,0:T(8,128)S(1)} %edges.1.edge_hbm), custom_call_target="tpu_custom_call" | custom-call | tf_op jit(solution)/shard_map/factors/pallas_call | solution.py:441
  35.7 0.0 collective-permute-done.e_ref
  35.7 5.1 %collide.1 = f32[16,32,256]{2,1,0:T(8,128)S(1)} custom-call(f32[16,72,128]{2,1,0:T(8,128)S(1)} %all-to-all-done.g_ref, f32[136,128]{1,0:T(8,128)S(1)} %collective-permute-done.e_ref, f32[36,128]{1,0:T(8,128)S(1)} %get-tuple-element.15.rate_in, bf16[2048,512]{1,0:T(8,128)(2,1)S(1)} %get-tuple-element.16.hi_ref, ...), custom_call_target="tpu_custom_call" | custom-call | tf_op jit(solution)/shard_map/collide/pallas_call | solution.py:454
  40.8 28.6 %all_to_all.10.t_ref = f32[16,32,256]{2,1,0:T(8,128)S(1)} all-to-all(f32[16,32,256]{2,1,0:T(8,128)S(1)} %collide.1), channel_id=1, replica_groups=mesh['vel'=16,'space'=64] {'vel'}, dimensions={0} | all-to-all | bytes 1048576 | tf_op jit(solution)/shard_map/all_to_all | solution.py:474
  69.4 0.9 %unflip.1 = f32[256,512]{1,0:T(8,128)} custom-call(f32[16,32,256]{2,1,0:T(8,128)S(1)} %all_to_all.10.t_ref), custom_call_target="tpu_custom_call" | custom-call | tf_op jit(solution)/shard_map/unflip/pallas_call | solution.py:475
  (1 shorter events, 0.0 us)
Async XLA Ops:
  0.0 19.1 %copy-start = (f32[96,2048]{1,0:T(8,128)S(1)}, f32[96,2048]{1,0:T(8,128)}, u32[]{:S(2)}) copy-start(f32[96,2048]{1,0:T(8,128)} %constant.4.clone.table_hbm) | copy-start | bytes 2359300
  0.0 34.1 %copy-start.1 = (f32[192,512]{1,0:T(8,128)S(1)}, f32[192,512]{1,0:T(8,128)}, u32[]{:S(2)}) copy-start(f32[192,512]{1,0:T(8,128)} %constant.5.clone.table_hbm) | copy-start | bytes 1179652
  0.0 22.4 %copy-start.4 = (f32[4]{0:T(128)S(1)}, f32[4]{0:T(128)}, u32[]{:S(2)}) copy-start(f32[4]{0:T(128)} %param.8) | copy-start | bytes 52
  0.0 22.4 %copy-start.3 = (s32[512]{0:T(512)S(1)}, s32[512]{0:T(512)}, u32[]{:S(2)}) copy-start(s32[512]{0:T(512)} %param.7) | copy-start | bytes 6148
  0.0 34.1 %copy-start.2 = (f32[512]{0:T(512)S(1)}, f32[512]{0:T(512)}, u32[]{:S(2)}) copy-start(f32[512]{0:T(512)} %param.9) | copy-start | bytes 6148
  2.6 29.5 %all-to-all-start = ((f32[16,72,128]{2,1,0:T(8,128)}), f32[16,72,128]{2,1,0:T(8,128)S(1)}, u32[]{:S(2)}, u32[]{:S(2)}) async-start(f32[16,72,128]{2,1,0:T(8,128)} %flip.1.sent_hbm), calls=%async_computation | async-start | bytes 1179648 | tf_op jit(solution)/shard_map/all_to_all | solution.py:394
  32.2 3.6 %collective-permute-start = (f32[136,128]{1,0:T(8,128)S(1)}, f32[136,128]{1,0:T(8,128)S(1)}, u32[]{:S(2)}, u32[]{:S(2)}) collective-permute-start(f32[136,128]{1,0:T(8,128)S(1)} %edges.1.edge_hbm), channel_id=1, source_target_pairs={{64,65},{65,64},{1,2},{2,1},{66,67},{67,66},{3,4},{4,3},{68,69},{6... | collective-permute-start | bytes 208904 | tf_op jit(solution)/shard_map/ppermute | solution.py:439

commit v6 on v5

--- a/solution.py
+++ b/solution.py
@@ -216,9 +216,11 @@
         store.wait()
 
 
-def factor_kernel(table_hbm, w_ref, edge_hbm, hi_ref, lo_ref, wp_ref, table, sem):
+def factor_kernel(table_hbm, w_ref, edge_hbm, thi_hbm, hi_ref, lo_ref, wp_ref, thi_ref, table, sem, load_sem):
     copy = pltpu.make_async_copy(table_hbm, table, sem)
     copy.start()
+    load = pltpu.make_async_copy(thi_hbm, thi_ref, load_sem)
+    load.start()
     source = lax.broadcasted_iota(jnp.int32, (K, K), 0)
     target = lax.broadcasted_iota(jnp.int32, (K, K), 1)
     mode = jnp.where(target < K // 2, 2 * target, 2 * target + 1 - K)
@@ -235,11 +237,12 @@
         return carry
 
     lax.fori_loop(0, A, body, 0)
+    load.wait()
 
 
 def collide_kernel(
-    g_ref, e_ref, rate_in, hi_ref, lo_ref, wp_ref, thi_hbm, tlo_hbm,
-    out_ref, a_ref, b_ref, r_ref, l_ref, c_ref, m_ref, s_ref, thi_ref, tlo_ref, sems,
+    g_ref, e_ref, rate_in, hi_ref, lo_ref, wp_ref, thi_ref, tlo_hbm,
+    out_ref, a_ref, b_ref, r_ref, l_ref, c_ref, m_ref, s_ref, tlo_ref, sems,
 ):
     blocks, rows, _ = g_ref.shape
     wide = rows // 2
@@ -250,10 +253,9 @@
     lane = lax.broadcasted_iota(jnp.int32, (1, 128), 1)
     spot = place(blocks)
     loads = []
-    for n in range(4):
-        rows = slice(n // 2 * half, (n // 2 + 1) * half)
-        source, target = ((thi_hbm, thi_ref), (tlo_hbm, tlo_ref))[n % 2]
-        loads.append(pltpu.make_async_copy(source.at[rows, :], target.at[rows, :], sems.at[n]))
+    for n in range(2):
+        rows = slice(n * half, (n + 1) * half)
+        loads.append(pltpu.make_async_copy(tlo_hbm.at[rows, :], tlo_ref.at[rows, :], sems.at[n]))
         loads[n].start()
     r_ref[...] = rate_in[...]
 
@@ -304,10 +306,11 @@
             hi, lo = split(coef * wp_ref[0:1, modes])
             m_ref[0:count, modes] = hi
             m_ref[at : at + count, modes] = lo
+        for s in range(2):
+            modes = slice(s * half, (s + 1) * half)
             right = m_ref[: 2 * at, modes]
             if count == wide:
-                loads[2 * s].wait()
-                loads[2 * s + 1].wait()
+                loads[s].wait()
             back = dot(right, thi_ref[modes, :])
             c_ref[:count, s * H : (s + 1) * H] = (
                 back[:count] + back[at : at + count] + dot(right[:at], tlo_ref[modes, :])[:count]
@@ -444,17 +447,22 @@
             jax.ShapeDtypeStruct((H, K), BF16),
             jax.ShapeDtypeStruct((H, K), BF16),
             jax.ShapeDtypeStruct((8, K), F32),
+            jax.ShapeDtypeStruct((K, H), BF16),
         ),
-        in_specs=[ANY, VMEM, ANY],
-        out_specs=(VMEM,) * 3,
-        scratch_shapes=[pltpu.VMEM((2 * (A + B), K), F32), pltpu.SemaphoreType.DMA],
-        compiler_params=params(12),
+        in_specs=[ANY, VMEM, ANY, ANY],
+        out_specs=(VMEM,) * 4,
+        scratch_shapes=[
+            pltpu.VMEM((2 * (A + B), K), F32),
+            pltpu.SemaphoreType.DMA,
+            pltpu.SemaphoreType.DMA,
+        ],
+        compiler_params=params(14),
         name="factors",
-    )(jnp.asarray(tables()), mode_weights[None, :], edge)
+    )(jnp.asarray(tables()), mode_weights[None, :], edge, by_modes[0])
     back = pl.pallas_call(
         collide_kernel,
         out_shape=jax.ShapeDtypeStruct((blocks, own, nv), F32),
-        in_specs=[VMEM] * 6 + [ANY] * 2,
+        in_specs=[VMEM] * 7 + [ANY],
         out_specs=VMEM,
         scratch_shapes=[
             pltpu.VMEM((V // 128, wide + 4, 128), F32),
@@ -465,12 +473,11 @@
             pltpu.VMEM((96, K), BF16),
             pltpu.VMEM((V // 128, 8, 128), F32),
             pltpu.VMEM((K, H), BF16),
-            pltpu.VMEM((K, H), BF16),
-            pltpu.SemaphoreType.DMA((4,)),
+            pltpu.SemaphoreType.DMA((2,)),
         ],
         compiler_params=params(24),
         name="collide",
-    )(got, edge_in, rate, *factors, *by_modes)
+    )(got, edge_in, rate, *factors, by_modes[1])
     result = lax.all_to_all(back, "vel", 0, 0, tiled=True)
     return pl.pallas_call(
         unflip_kernel,

time: 70.6 us -> 70 us (level)
  Pallas kernels: 14.3 us -> 13.5 us
    pallas_call x1, Pallas kernels: 5.1 us -> 4.08 us  [shards(): pl.pallas_call(collide_kernel, out_shape=jax.ShapeDtypeStruct((blocks, ow...]
where the time goes in v6:
time: 70 us; the launch traced here: 69.7 us
  blocking collectives  28.7 us (41%)
  starting transfers between devices  18.4 us (26%)
  Pallas kernels  13.5 us (19%)
  waiting for transfers between devices  8.99 us (13%)
    all_to_all x1, blocking collectives, shards(): result = lax.all_to_all(back, 'vel', 0, 0, tiled=True)  28.7 us
    all_to_all x1, starting transfers between devices, shards(): got = lax.all_to_all(sent, 'vel', 0, 0, tiled=True)  16.4 us
    all_to_all x1, waiting for transfers between devices, shards(): got = lax.all_to_all(sent, 'vel', 0, 0, tiled=True)  8.98 us
    pallas_call x1, Pallas kernels, shards(): pl.pallas_call(collide_kernel, out_shape=jax.ShapeDtypeStruct((blocks, ow...  4.08 us
    pallas_call x1, Pallas kernels, shards(): pl.pallas_call(mode_factor_kernel, out_shape=(pltpu.MemorySpace.HBM((K, H...  3.34 us
    pallas_call x1, Pallas kernels, shards(): pl.pallas_call(functools.partial(flip_kernel, blocks), out_shape=jax.Shap...  2.61 us
    ppermute x1, starting transfers between devices, shards(): edge_in = lax.ppermute(edge, ('vel', 'space'), pairs)  1.92 us
    pallas_call x1, Pallas kernels, shards(): pl.pallas_call(factor_kernel, out_shape=(jax.ShapeDtypeStruct((H, K), BF1...  1.8 us
  transfers between devices with their start and end apart: 2, of which 1 were waited for; matrix products, arithmetic and copies ran while one was open for 0% of the time, Pallas kernels for 8%

profile of v6, /device:TPU:8, one launch (start us, length us, event | category | flops | bytes accessed | tf_op | source)
XLA Modules:
  0.0 69.7 jit_solution(6419288073548770821)
XLA Ops:
  0.0 0.0 copy-start
  0.0 0.0 copy-start.1
  0.0 0.0 copy-start.4
  0.0 0.0 copy-start.2
  0.0 0.0 copy-start.3
  0.0 2.6 %flip.1.sent_hbm = f32[16,72,128]{2,1,0:T(8,128)} custom-call(f32[256,512]{1,0:T(8,128)} %f_hbm.1), custom_call_target="tpu_custom_call" | custom-call | tf_op jit(solution)/shard_map/flip/pallas_call | solution.py:382
  2.6 16.4 %all-to-all-start = ((f32[16,72,128]{2,1,0:T(8,128)}), f32[16,72,128]{2,1,0:T(8,128)S(1)}, u32[]{:S(2)}, u32[]{:S(2)}) async-start(f32[16,72,128]{2,1,0:T(8,128)} %flip.1.sent_hbm), calls=%async_computation | async-start | bytes 1179648 | tf_op jit(solution)/shard_map/all_to_all | solution.py:397
  19.1 0.0 copy-done
  19.1 3.3 %mode_factors.1 = (bf16[512,2048]{1,0:T(8,128)(2,1)}, bf16[512,2048]{1,0:T(8,128)(2,1)}, f32[8,128]{1,0:T(8,128)S(1)}) custom-call(f32[96,2048]{1,0:T(8,128)S(1)} %copy-done, f32[16,72,128]{2,1,0:T(8,128)} %flip.1.sent_hbm), custom_call_target="tpu_custom_call" | custom-call | tf_op jit(solution)/shard_map/mode_factors/pallas_call | solution.py:410
  22.4 0.0 copy-done.4
  22.4 0.0 copy-done.2
  22.5 0.7 rates.1
  23.1 9.0 %all-to-all-done.g_ref = f32[16,72,128]{2,1,0:T(8,128)S(1)} async-done(((f32[16,72,128]{2,1,0:T(8,128)}), f32[16,72,128]{2,1,0:T(8,128)S(1)}, u32[]{:S(2)}, u32[]{:S(2)}) %all-to-all-start) | async-done | bytes 589856 | tf_op jit(solution)/shard_map/all_to_all | solution.py:397
  32.2 1.9 %collective-permute-start = (f32[136,128]{1,0:T(8,128)S(1)}, f32[136,128]{1,0:T(8,128)S(1)}, u32[]{:S(2)}, u32[]{:S(2)}) collective-permute-start(f32[136,128]{1,0:T(8,128)S(1)} %edges.1.edge_hbm), channel_id=1, source_target_pairs={{64,65},{65,64},{1,2},{2,1},{66,67},{67,66},{3,4},{4,3},{68,69},{6... | collective-permute-start | bytes 208904 | tf_op jit(solution)/shard_map/ppermute | solution.py:442
  34.1 0.0 copy-done.1
  34.1 0.0 copy-done.3
  34.1 1.8 %factors.1 = (bf16[2048,512]{1,0:T(8,128)(2,1)S(1)}, bf16[2048,512]{1,0:T(8,128)(2,1)S(1)}, f32[8,512]{1,0:T(8,128)S(1)}, bf16[512,2048]{1,0:T(8,128)(2,1)S(1)}) custom-call(f32[192,512]{1,0:T(8,128)S(1)} %copy-done.1, f32[1,512]{1,0:T(1,128)S(1)} %bitcast.4, f32[136,128]{1,0:T(8,128)S(1)} %edges.1.edge_hbm, bf16[512,2048]{1,0:T(8,128)(2,1)} %get-tuple-element.17.thi_hbm), custom_call_target="tpu_custom_call" | custom-call | tf_op jit(solution)/shard_map/factors/pallas_call | solution.py:444
  35.9 0.0 collective-permute-done.e_ref
  35.9 4.1 %collide.1 = f32[16,32,256]{2,1,0:T(8,128)S(1)} custom-call(f32[16,72,128]{2,1,0:T(8,128)S(1)} %all-to-all-done.g_ref, f32[136,128]{1,0:T(8,128)S(1)} %collective-permute-done.e_ref, f32[36,128]{1,0:T(8,128)S(1)} %get-tuple-element.16.rate_in, bf16[2048,512]{1,0:T(8,128)(2,1)S(1)} %get-tuple-element.18.hi_ref, ...), custom_call_target="tpu_custom_call" | custom-call | tf_op jit(solution)/shard_map/collide/pallas_call | solution.py:462
  40.0 28.7 %all_to_all.10.t_ref = f32[16,32,256]{2,1,0:T(8,128)S(1)} all-to-all(f32[16,32,256]{2,1,0:T(8,128)S(1)} %collide.1), channel_id=1, replica_groups=mesh['vel'=16,'space'=64] {'vel'}, dimensions={0} | all-to-all | bytes 1048576 | tf_op jit(solution)/shard_map/all_to_all | solution.py:481
  68.8 0.9 %unflip.1 = f32[256,512]{1,0:T(8,128)} custom-call(f32[16,32,256]{2,1,0:T(8,128)S(1)} %all_to_all.10.t_ref), custom_call_target="tpu_custom_call" | custom-call | tf_op jit(solution)/shard_map/unflip/pallas_call | solution.py:482
  (1 shorter events, 0.0 us)
Async XLA Ops:
  0.0 19.1 %copy-start = (f32[96,2048]{1,0:T(8,128)S(1)}, f32[96,2048]{1,0:T(8,128)}, u32[]{:S(2)}) copy-start(f32[96,2048]{1,0:T(8,128)} %constant.4.clone.table_hbm) | copy-start | bytes 2359300
  0.0 34.1 %copy-start.1 = (f32[192,512]{1,0:T(8,128)S(1)}, f32[192,512]{1,0:T(8,128)}, u32[]{:S(2)}) copy-start(f32[192,512]{1,0:T(8,128)} %constant.5.clone.table_hbm) | copy-start | bytes 1179652
  0.0 22.4 %copy-start.4 = (f32[4]{0:T(128)S(1)}, f32[4]{0:T(128)}, u32[]{:S(2)}) copy-start(f32[4]{0:T(128)} %param.8) | copy-start | bytes 52
  0.0 22.4 %copy-start.2 = (s32[512]{0:T(512)S(1)}, s32[512]{0:T(512)}, u32[]{:S(2)}) copy-start(s32[512]{0:T(512)} %param.7) | copy-start | bytes 6148
  0.0 34.1 %copy-start.3 = (f32[512]{0:T(512)S(1)}, f32[512]{0:T(512)}, u32[]{:S(2)}) copy-start(f32[512]{0:T(512)} %param.9) | copy-start | bytes 6148
  2.6 29.5 %all-to-all-start = ((f32[16,72,128]{2,1,0:T(8,128)}), f32[16,72,128]{2,1,0:T(8,128)S(1)}, u32[]{:S(2)}, u32[]{:S(2)}) async-start(f32[16,72,128]{2,1,0:T(8,128)} %flip.1.sent_hbm), calls=%async_computation | async-start | bytes 1179648 | tf_op jit(solution)/shard_map/all_to_all | solution.py:397
  32.2 3.8 %collective-permute-start = (f32[136,128]{1,0:T(8,128)S(1)}, f32[136,128]{1,0:T(8,128)S(1)}, u32[]{:S(2)}, u32[]{:S(2)}) collective-permute-start(f32[136,128]{1,0:T(8,128)S(1)} %edges.1.edge_hbm), channel_id=1, source_target_pairs={{64,65},{65,64},{1,2},{2,1},{66,67},{67,66},{3,4},{4,3},{68,69},{6... | collective-permute-start | bytes 208904 | tf_op jit(solution)/shard_map/ppermute | solution.py:442

commit v7 on v5

--- a/solution.py
+++ b/solution.py
@@ -304,6 +304,8 @@
             hi, lo = split(coef * wp_ref[0:1, modes])
             m_ref[0:count, modes] = hi
             m_ref[at : at + count, modes] = lo
+        for s in range(2):
+            modes = slice(s * half, (s + 1) * half)
             right = m_ref[: 2 * at, modes]
             if count == wide:
                 loads[2 * s].wait()

time: 70.6 us -> 70.3 us (level)
  no operation moved by 1% of the time
where the time goes in v7:
time: 70.3 us; the launch traced here: 70 us
  blocking collectives  28.8 us (41%)
  starting transfers between devices  18.4 us (26%)
  Pallas kernels  13.8 us (20%)
  waiting for transfers between devices  8.99 us (13%)
    all_to_all x1, blocking collectives, shards(): result = lax.all_to_all(back, 'vel', 0, 0, tiled=True)  28.8 us
    all_to_all x1, starting transfers between devices, shards(): got = lax.all_to_all(sent, 'vel', 0, 0, tiled=True)  16.4 us
    all_to_all x1, waiting for transfers between devices, shards(): got = lax.all_to_all(sent, 'vel', 0, 0, tiled=True)  8.98 us
    pallas_call x1, Pallas kernels, shards(): pl.pallas_call(collide_kernel, out_shape=jax.ShapeDtypeStruct((blocks, ow...  4.59 us
    pallas_call x1, Pallas kernels, shards(): pl.pallas_call(mode_factor_kernel, out_shape=(pltpu.MemorySpace.HBM((K, H...  3.34 us
    pallas_call x1, Pallas kernels, shards(): pl.pallas_call(functools.partial(flip_kernel, blocks), out_shape=jax.Shap...  2.61 us
    ppermute x1, starting transfers between devices, shards(): edge_in = lax.ppermute(edge, ('vel', 'space'), pairs)  1.92 us
    pallas_call x1, Pallas kernels, shards(): pl.pallas_call(factor_kernel, out_shape=(jax.ShapeDtypeStruct((H, K), BF1...  1.6 us
  transfers between devices with their start and end apart: 2, of which 1 were waited for; matrix products, arithmetic and copies ran while one was open for 0% of the time, Pallas kernels for 8%

profile of v7, /device:TPU:8, one launch (start us, length us, event | category | flops | bytes accessed | tf_op | source)
XLA Modules:
  0.0 70.0 jit_solution(4361385802468404555)
XLA Ops:
  0.0 0.0 copy-start
  0.0 0.0 copy-start.1
  0.0 0.0 copy-start.4
  0.0 0.0 copy-start.3
  0.0 0.0 copy-start.2
  0.0 2.6 %flip.1.sent_hbm = f32[16,72,128]{2,1,0:T(8,128)} custom-call(f32[256,512]{1,0:T(8,128)} %f_hbm.1), custom_call_target="tpu_custom_call" | custom-call | tf_op jit(solution)/shard_map/flip/pallas_call | solution.py:381
  2.6 16.4 %all-to-all-start = ((f32[16,72,128]{2,1,0:T(8,128)}), f32[16,72,128]{2,1,0:T(8,128)S(1)}, u32[]{:S(2)}, u32[]{:S(2)}) async-start(f32[16,72,128]{2,1,0:T(8,128)} %flip.1.sent_hbm), calls=%async_computation | async-start | bytes 1179648 | tf_op jit(solution)/shard_map/all_to_all | solution.py:396
  19.1 0.0 copy-done
  19.1 3.3 %mode_factors.1 = (bf16[512,2048]{1,0:T(8,128)(2,1)}, bf16[512,2048]{1,0:T(8,128)(2,1)}, f32[8,128]{1,0:T(8,128)S(1)}) custom-call(f32[96,2048]{1,0:T(8,128)S(1)} %copy-done, f32[16,72,128]{2,1,0:T(8,128)} %flip.1.sent_hbm), custom_call_target="tpu_custom_call" | custom-call | tf_op jit(solution)/shard_map/mode_factors/pallas_call | solution.py:409
  22.4 0.0 copy-done.4
  22.4 0.0 copy-done.3
  22.5 0.7 rates.1
  23.1 9.0 %all-to-all-done.g_ref = f32[16,72,128]{2,1,0:T(8,128)S(1)} async-done(((f32[16,72,128]{2,1,0:T(8,128)}), f32[16,72,128]{2,1,0:T(8,128)S(1)}, u32[]{:S(2)}, u32[]{:S(2)}) %all-to-all-start) | async-done | bytes 589856 | tf_op jit(solution)/shard_map/all_to_all | solution.py:396
  32.2 1.9 %collective-permute-start = (f32[136,128]{1,0:T(8,128)S(1)}, f32[136,128]{1,0:T(8,128)S(1)}, u32[]{:S(2)}, u32[]{:S(2)}) collective-permute-start(f32[136,128]{1,0:T(8,128)S(1)} %edges.1.edge_hbm), channel_id=1, source_target_pairs={{64,65},{65,64},{1,2},{2,1},{66,67},{67,66},{3,4},{4,3},{68,69},{6... | collective-permute-start | bytes 208904 | tf_op jit(solution)/shard_map/ppermute | solution.py:441
  34.1 0.0 copy-done.1
  34.1 0.0 copy-done.2
  34.1 1.6 %factors.1 = (bf16[2048,512]{1,0:T(8,128)(2,1)S(1)}, bf16[2048,512]{1,0:T(8,128)(2,1)S(1)}, f32[8,512]{1,0:T(8,128)S(1)}) custom-call(f32[192,512]{1,0:T(8,128)S(1)} %copy-done.1, f32[1,512]{1,0:T(1,128)S(1)} %bitcast.3, f32[136,128]{1,0:T(8,128)S(1)} %edges.1.edge_hbm), custom_call_target="tpu_custom_call" | custom-call | tf_op jit(solution)/shard_map/factors/pallas_call | solution.py:443
  35.7 0.0 collective-permute-done.e_ref
  35.7 4.6 %collide.1 = f32[16,32,256]{2,1,0:T(8,128)S(1)} custom-call(f32[16,72,128]{2,1,0:T(8,128)S(1)} %all-to-all-done.g_ref, f32[136,128]{1,0:T(8,128)S(1)} %collective-permute-done.e_ref, f32[36,128]{1,0:T(8,128)S(1)} %get-tuple-element.15.rate_in, bf16[2048,512]{1,0:T(8,128)(2,1)S(1)} %get-tuple-element.16.hi_ref, ...), custom_call_target="tpu_custom_call" | custom-call | tf_op jit(solution)/shard_map/collide/pallas_call | solution.py:456
  40.3 28.8 %all_to_all.10.t_ref = f32[16,32,256]{2,1,0:T(8,128)S(1)} all-to-all(f32[16,32,256]{2,1,0:T(8,128)S(1)} %collide.1), channel_id=1, replica_groups=mesh['vel'=16,'space'=64] {'vel'}, dimensions={0} | all-to-all | bytes 1048576 | tf_op jit(solution)/shard_map/all_to_all | solution.py:476
  69.1 0.9 %unflip.1 = f32[256,512]{1,0:T(8,128)} custom-call(f32[16,32,256]{2,1,0:T(8,128)S(1)} %all_to_all.10.t_ref), custom_call_target="tpu_custom_call" | custom-call | tf_op jit(solution)/shard_map/unflip/pallas_call | solution.py:477
  (1 shorter events, 0.0 us)
Async XLA Ops:
  0.0 19.1 %copy-start = (f32[96,2048]{1,0:T(8,128)S(1)}, f32[96,2048]{1,0:T(8,128)}, u32[]{:S(2)}) copy-start(f32[96,2048]{1,0:T(8,128)} %constant.4.clone.table_hbm) | copy-start | bytes 2359300
  0.0 34.1 %copy-start.1 = (f32[192,512]{1,0:T(8,128)S(1)}, f32[192,512]{1,0:T(8,128)}, u32[]{:S(2)}) copy-start(f32[192,512]{1,0:T(8,128)} %constant.5.clone.table_hbm) | copy-start | bytes 1179652
  0.0 22.4 %copy-start.4 = (f32[4]{0:T(128)S(1)}, f32[4]{0:T(128)}, u32[]{:S(2)}) copy-start(f32[4]{0:T(128)} %param.8) | copy-start | bytes 52
  0.0 22.4 %copy-start.3 = (s32[512]{0:T(512)S(1)}, s32[512]{0:T(512)}, u32[]{:S(2)}) copy-start(s32[512]{0:T(512)} %param.7) | copy-start | bytes 6148
  0.0 34.1 %copy-start.2 = (f32[512]{0:T(512)S(1)}, f32[512]{0:T(512)}, u32[]{:S(2)}) copy-start(f32[512]{0:T(512)} %param.9) | copy-start | bytes 6148
  2.6 29.5 %all-to-all-start = ((f32[16,72,128]{2,1,0:T(8,128)}), f32[16,72,128]{2,1,0:T(8,128)S(1)}, u32[]{:S(2)}, u32[]{:S(2)}) async-start(f32[16,72,128]{2,1,0:T(8,128)} %flip.1.sent_hbm), calls=%async_computation | async-start | bytes 1179648 | tf_op jit(solution)/shard_map/all_to_all | solution.py:396
  32.2 3.6 %collective-permute-start = (f32[136,128]{1,0:T(8,128)S(1)}, f32[136,128]{1,0:T(8,128)S(1)}, u32[]{:S(2)}, u32[]{:S(2)}) collective-permute-start(f32[136,128]{1,0:T(8,128)S(1)} %edges.1.edge_hbm), channel_id=1, source_target_pairs={{64,65},{65,64},{1,2},{2,1},{66,67},{67,66},{3,4},{4,3},{68,69},{6... | collective-permute-start | bytes 208904 | tf_op jit(solution)/shard_map/ppermute | solution.py:441
